TPU v7x, 32 devices: a whole 2x2x4 slice. The times are simulated.
32 devices in a mesh: dp: 8 (over z, x), seq: 4 (over y, core).
Axes of the slice: x: 2, y: 2, z: 4, core: 2. Of those that a mesh axis runs over, the one named last changes fastest.
Arguments:
- inputs: bfloat16 [16, 2048, 768], P('dp', 'seq'), may hold values from -6 to 6
- lengths: int32 [16], P('dp'), may hold values from 256 to 2048
- first_gain: float32 [768], replicated, may hold values from 0.5 to 1.5
- first_shift: float32 [768], replicated, may hold values from -2 to 2
- query_weight: bfloat16 [768, 768], replicated, may hold values from -0.21875 to 0.21875
- query_bias: float32 [768], replicated, may hold values from -1.5 to 1.5
- key_weight: bfloat16 [768, 768], replicated, may hold values from -0.21875 to 0.21875
- value_weight: bfloat16 [768, 768], replicated, may hold values from -0.21875 to 0.21875
- value_bias: float32 [768], replicated, may hold values from -0.25 to 0.25
- output_weight: bfloat16 [768, 768], replicated, may hold values from -4 to 4
- output_bias: float32 [768], replicated, may hold values from -2 to 2
- second_gain: float32 [768], replicated, may hold values from 0.5 to 1.5
- second_shift: float32 [768], replicated, may hold values from -2 to 2
- inner_weight: bfloat16 [768, 3072], replicated, may hold values from -0.21875 to 0.21875
- inner_bias: float32 [3072], replicated, may hold values from -2 to 2
- outer_weight: bfloat16 [3072, 768], replicated, may hold values from -0.109375 to 0.109375
- outer_bias: float32 [768], replicated, may hold values from -2 to 2
- cotangent: bfloat16 [16, 2048, 768], P('dp', 'seq'), may hold values from -6 to 6
Outputs:
- result: bfloat16 [16, 2048, 768], P('dp', 'seq')
- grad_inputs: bfloat16 [16, 2048, 768], P('dp', 'seq')
- grad_first_gain: float32 [768], replicated
- grad_first_shift: float32 [768], replicated
- grad_query_weight: float32 [768, 768], P('dp')
- grad_query_bias: float32 [768], replicated
- grad_key_weight: float32 [768, 768], P('dp')
- grad_value_weight: float32 [768, 768], P('dp')
- grad_value_bias: float32 [768], replicated
- grad_output_weight: float32 [768, 768], P('dp')
- grad_output_bias: float32 [768], replicated
- grad_second_gain: float32 [768], replicated
- grad_second_shift: float32 [768], replicated
- grad_inner_weight: float32 [768, 3072], P('dp')
- grad_inner_bias: float32 [3072], replicated
- grad_outer_weight: float32 [3072, 768], P('dp')
- grad_outer_bias: float32 [768], replicated
- stream_scale: float32 [], replicated
- attention_scale: float32 [], replicated
- feedforward_scale: float32 [], replicated
All inputs are finite; a program needn't handle non-finite values.
Results may differ from a plain program's by a relative error of at most 0.012.
Values may be sent and summed in bfloat16 or wider, within the bound.
A program may use at most 256 MiB of HBM per device.

v0:
```python
import jax
import jax.numpy as jnp
from jax import lax
from jax.sharding import PartitionSpec as P

HEADS = 12
HEAD_DIM = 64


EPSILON = 1e-12
NEGATIVE = -1e30


def norm_apply(values, gain_vec, shift_vec):
    average = jnp.mean(values, axis=-1, keepdims=True)
    centered = values - average
    spread = jnp.mean(centered * centered, axis=-1, keepdims=True)
    return centered * lax.rsqrt(spread + EPSILON) * gain_vec + shift_vec


def exact_gelu(values):
    return jax.nn.gelu(values, approximate=False)


def local(
    inputs,
    lengths,
    first_gain,
    first_shift,
    query_weight,
    query_bias,
    key_weight,
    value_weight,
    value_bias,
    output_weight,
    output_bias,
    second_gain,
    second_shift,
    inner_weight,
    inner_bias,
    outer_weight,
    outer_bias,
    cotangent,
):
    groups = lax.axis_size("seq")
    seq_count, local_len, model_width = inputs.shape
    full_len = local_len * groups
    heads_here = HEADS // groups
    tokens_here = seq_count * local_len
    score_scale = HEAD_DIM ** (-0.5)
    block_rows = min(512, full_len)
    block_count = full_len // block_rows
    positions = lax.axis_index("seq") * local_len + jnp.arange(local_len, dtype=jnp.int32)
    valid_rows = positions[None, :] < lengths[:, None]
    keep_rows = valid_rows.reshape(tokens_here, 1).astype(jnp.float32)
    key_valid = jnp.arange(full_len, dtype=jnp.int32)[None, :] < lengths[:, None]
    flat_in = inputs.reshape(tokens_here, model_width).astype(jnp.float32)

    def to_heads(flat):
        return flat.reshape(seq_count, local_len, groups, model_width // groups)

    head_shape = (seq_count, full_len, heads_here, HEAD_DIM)
    merged_shape = (seq_count, full_len, 1, heads_here * HEAD_DIM)
    normed_one, norm_one_back = jax.vjp(norm_apply, flat_in, first_gain, first_shift)
    normed_one_low = normed_one.astype(jnp.bfloat16)
    queries = (
        jnp.dot(normed_one_low, query_weight, preferred_element_type=jnp.float32) + query_bias
    ).astype(jnp.bfloat16)
    keys_local = jnp.dot(normed_one_low, key_weight, preferred_element_type=jnp.float32).astype(
        jnp.bfloat16
    )
    values_local = (
        jnp.dot(normed_one_low, value_weight, preferred_element_type=jnp.float32) + value_bias
    ).astype(jnp.bfloat16)
    head_q, head_k, head_v = (
        lax.all_to_all(to_heads(queries), "seq", split_axis=2, concat_axis=1, tiled=True),
        lax.all_to_all(to_heads(keys_local), "seq", split_axis=2, concat_axis=1, tiled=True),
        lax.all_to_all(to_heads(values_local), "seq", split_axis=2, concat_axis=1, tiled=True),
    )
    head_q = head_q.reshape(head_shape)
    head_k = head_k.reshape(head_shape)
    head_v = head_v.reshape(head_shape)

    def scores_of(query_blk):
        raw_scores = (
            jnp.einsum("sqhd,skhd->shqk", query_blk, head_k, preferred_element_type=jnp.float32)
            * score_scale
        )
        return jnp.where(key_valid[:, None, None, :], raw_scores, NEGATIVE)

    def forward_block(block_index, carry):
        outputs, log_sums = carry
        offset = block_index * block_rows
        query_blk = lax.dynamic_slice_in_dim(head_q, offset, block_rows, 1)
        logits = scores_of(query_blk)
        row_max = jnp.max(logits, axis=-1, keepdims=True)
        row_total = jnp.sum(jnp.exp(logits - row_max), axis=-1, keepdims=True)
        log_sum = row_max + jnp.log(row_total)
        probability_low = jnp.exp(logits - log_sum).astype(jnp.bfloat16)
        mixed_heads = jnp.einsum(
            "shqk,skhd->sqhd", probability_low, head_v, preferred_element_type=jnp.float32
        ).astype(jnp.bfloat16)
        outputs = lax.dynamic_update_slice_in_dim(outputs, mixed_heads, offset, 1)
        log_sums = lax.dynamic_update_slice_in_dim(log_sums, log_sum[..., 0], offset, 2)
        return (outputs, log_sums)

    empty_out = jnp.zeros(head_shape, jnp.bfloat16)
    empty_sums = jnp.zeros((seq_count, heads_here, full_len), jnp.float32)
    head_out, log_sums = lax.fori_loop(0, block_count, forward_block, (empty_out, empty_sums))
    attended = lax.all_to_all(
        head_out.reshape(merged_shape), "seq", split_axis=1, concat_axis=2, tiled=True
    ).reshape(tokens_here, model_width)
    branch_attn = jnp.dot(attended, output_weight, preferred_element_type=jnp.float32) + output_bias
    hidden = flat_in + branch_attn
    normed_two, norm_two_back = jax.vjp(norm_apply, hidden, second_gain, second_shift)
    normed_two_low = normed_two.astype(jnp.bfloat16)
    inner = jnp.dot(normed_two_low, inner_weight, preferred_element_type=jnp.float32) + inner_bias
    activated_full, gelu_back = jax.vjp(exact_gelu, inner)
    activated = activated_full.astype(jnp.bfloat16)
    branch_ffn = jnp.dot(activated, outer_weight, preferred_element_type=jnp.float32) + outer_bias
    stream = keep_rows * (hidden + branch_ffn)
    result = stream.astype(jnp.bfloat16).reshape(inputs.shape)
    grad_stream = keep_rows * cotangent.reshape(tokens_here, model_width).astype(jnp.float32)
    grad_ffn_low = grad_stream.astype(jnp.bfloat16)
    grad_outer_weight = jnp.einsum(
        "tf,td->fd", activated, grad_ffn_low, preferred_element_type=jnp.float32
    )
    grad_outer_bias = jnp.sum(grad_ffn_low, axis=0, dtype=jnp.float32)
    grad_activated = jnp.einsum(
        "td,fd->tf", grad_ffn_low, outer_weight, preferred_element_type=jnp.float32
    )
    grad_inner_low = gelu_back(grad_activated)[0].astype(jnp.bfloat16)
    grad_inner_weight = jnp.einsum(
        "td,tf->df", normed_two_low, grad_inner_low, preferred_element_type=jnp.float32
    )
    grad_inner_bias = jnp.sum(grad_inner_low, axis=0, dtype=jnp.float32)
    grad_normed_two = jnp.einsum(
        "tf,df->td", grad_inner_low, inner_weight, preferred_element_type=jnp.float32
    )
    grad_hidden_norm, grad_second_gain, grad_second_shift = norm_two_back(grad_normed_two)
    grad_hidden = grad_stream + grad_hidden_norm
    grad_attn_low = grad_hidden.astype(jnp.bfloat16)
    grad_output_weight = jnp.einsum(
        "tc,td->cd", attended, grad_attn_low, preferred_element_type=jnp.float32
    )
    grad_output_bias = jnp.sum(grad_attn_low, axis=0, dtype=jnp.float32)
    grad_attended = jnp.einsum(
        "td,cd->tc", grad_attn_low, output_weight, preferred_element_type=jnp.float32
    ).astype(jnp.bfloat16)
    grad_heads = lax.all_to_all(
        to_heads(grad_attended), "seq", split_axis=2, concat_axis=1, tiled=True
    ).reshape(head_shape)

    def backward_block(block_index, carry):
        grad_q_all, grad_k_acc, grad_v_acc = carry
        offset = block_index * block_rows
        query_blk = lax.dynamic_slice_in_dim(head_q, offset, block_rows, 1)
        grad_out_blk = lax.dynamic_slice_in_dim(grad_heads, offset, block_rows, 1)
        log_sum = lax.dynamic_slice_in_dim(log_sums, offset, block_rows, 2)
        probability = jnp.exp(scores_of(query_blk) - log_sum[..., None])
        probability_low = probability.astype(jnp.bfloat16)
        grad_prob = jnp.einsum(
            "sqhd,skhd->shqk", grad_out_blk, head_v, preferred_element_type=jnp.float32
        )
        row_sums = jnp.sum(probability * grad_prob, axis=-1, keepdims=True)
        grad_scores = (probability * (grad_prob - row_sums)).astype(jnp.bfloat16)
        grad_q_blk = (
            jnp.einsum("shqk,skhd->sqhd", grad_scores, head_k, preferred_element_type=jnp.float32)
            * score_scale
        ).astype(jnp.bfloat16)
        grad_q_all = lax.dynamic_update_slice_in_dim(grad_q_all, grad_q_blk, offset, 1)
        grad_k_acc = (
            grad_k_acc
            + jnp.einsum(
                "shqk,sqhd->skhd", grad_scores, query_blk, preferred_element_type=jnp.float32
            )
            * score_scale
        )
        grad_v_acc = grad_v_acc + jnp.einsum(
            "shqk,sqhd->skhd", probability_low, grad_out_blk, preferred_element_type=jnp.float32
        )
        return (grad_q_all, grad_k_acc, grad_v_acc)

    zeros_low = jnp.zeros(head_shape, jnp.bfloat16)
    zeros_full = jnp.zeros(head_shape, jnp.float32)
    grad_q_head, grad_k_head, grad_v_head = lax.fori_loop(
        0, block_count, backward_block, (zeros_low, zeros_full, zeros_full)
    )
    grad_q_tok, grad_k_tok, grad_v_tok = (
        lax.all_to_all(
            grad_q_head.reshape(merged_shape), "seq", split_axis=1, concat_axis=2, tiled=True
        ),
        lax.all_to_all(
            grad_k_head.astype(jnp.bfloat16).reshape(merged_shape),
            "seq",
            split_axis=1,
            concat_axis=2,
            tiled=True,
        ),
        lax.all_to_all(
            grad_v_head.astype(jnp.bfloat16).reshape(merged_shape),
            "seq",
            split_axis=1,
            concat_axis=2,
            tiled=True,
        ),
    )
    grad_q_tok = grad_q_tok.reshape(tokens_here, model_width)
    grad_k_tok = grad_k_tok.reshape(tokens_here, model_width)
    grad_v_tok = grad_v_tok.reshape(tokens_here, model_width)
    grad_query_weight = jnp.einsum(
        "td,te->de", normed_one_low, grad_q_tok, preferred_element_type=jnp.float32
    )
    grad_key_weight = jnp.einsum(
        "td,te->de", normed_one_low, grad_k_tok, preferred_element_type=jnp.float32
    )
    grad_value_weight = jnp.einsum(
        "td,te->de", normed_one_low, grad_v_tok, preferred_element_type=jnp.float32
    )
    grad_query_bias = jnp.sum(grad_q_tok, axis=0, dtype=jnp.float32)
    grad_value_bias = jnp.sum(grad_v_tok, axis=0, dtype=jnp.float32)
    grad_normed_one = (
        jnp.einsum("te,de->td", grad_q_tok, query_weight, preferred_element_type=jnp.float32)
        + jnp.einsum("te,de->td", grad_k_tok, key_weight, preferred_element_type=jnp.float32)
        + jnp.einsum("te,de->td", grad_v_tok, value_weight, preferred_element_type=jnp.float32)
    )
    grad_in_norm, grad_first_gain, grad_first_shift = norm_one_back(grad_normed_one)
    grad_inputs = (grad_hidden + grad_in_norm).astype(jnp.bfloat16).reshape(inputs.shape)
    totals = lax.psum(
        (
            jnp.sum(stream * stream),
            jnp.sum(keep_rows * branch_attn * branch_attn),
            jnp.sum(keep_rows * branch_ffn * branch_ffn),
            jnp.sum(keep_rows),
            grad_first_gain,
            grad_first_shift,
            grad_query_bias,
            grad_value_bias,
            grad_output_bias,
            grad_second_gain,
            grad_second_shift,
            grad_inner_bias,
            grad_outer_bias,
        ),
        ("dp", "seq"),
    )
    denominator = totals[3] * model_width
    stream_scale = jnp.sqrt(totals[0] / denominator)
    attention_scale = jnp.sqrt(totals[1] / denominator)
    feedforward_scale = jnp.sqrt(totals[2] / denominator)
    data_groups = lax.axis_size("dp")
    pieces = (
        lax.psum_scatter(
            grad_query_weight.reshape(-1), ("dp", "seq"), scatter_dimension=0, tiled=True
        ),
        lax.psum_scatter(
            grad_key_weight.reshape(-1), ("dp", "seq"), scatter_dimension=0, tiled=True
        ),
        lax.psum_scatter(
            grad_value_weight.reshape(-1), ("dp", "seq"), scatter_dimension=0, tiled=True
        ),
        lax.psum_scatter(
            grad_output_weight.reshape(-1), ("dp", "seq"), scatter_dimension=0, tiled=True
        ),
        lax.psum_scatter(
            grad_inner_weight.reshape(-1), ("dp", "seq"), scatter_dimension=0, tiled=True
        ),
        lax.psum_scatter(
            grad_outer_weight.reshape(-1), ("dp", "seq"), scatter_dimension=0, tiled=True
        ),
    )
    joined = (
        lax.all_gather(pieces[0].astype(jnp.bfloat16), "seq", axis=0, tiled=True).astype(
            jnp.float32
        ),
        lax.all_gather(pieces[1].astype(jnp.bfloat16), "seq", axis=0, tiled=True).astype(
            jnp.float32
        ),
        lax.all_gather(pieces[2].astype(jnp.bfloat16), "seq", axis=0, tiled=True).astype(
            jnp.float32
        ),
        lax.all_gather(pieces[3].astype(jnp.bfloat16), "seq", axis=0, tiled=True).astype(
            jnp.float32
        ),
        lax.all_gather(pieces[4].astype(jnp.bfloat16), "seq", axis=0, tiled=True).astype(
            jnp.float32
        ),
        lax.all_gather(pieces[5].astype(jnp.bfloat16), "seq", axis=0, tiled=True).astype(
            jnp.float32
        ),
    )
    summed_query = joined[0].reshape(model_width // data_groups, model_width)
    summed_key = joined[1].reshape(model_width // data_groups, model_width)
    summed_value = joined[2].reshape(model_width // data_groups, model_width)
    summed_output = joined[3].reshape(model_width // data_groups, model_width)
    summed_inner = joined[4].reshape(model_width // data_groups, inner_weight.shape[1])
    summed_outer = joined[5].reshape(outer_weight.shape[0] // data_groups, model_width)
    return (
        result,
        grad_inputs,
        totals[4],
        totals[5],
        summed_query,
        totals[6],
        summed_key,
        summed_value,
        totals[7],
        summed_output,
        totals[8],
        totals[9],
        totals[10],
        summed_inner,
        totals[11],
        summed_outer,
        totals[12],
        stream_scale,
        attention_scale,
        feedforward_scale,
    )


def solution(mesh):
    return jax.shard_map(
        local,
        mesh=mesh,
        in_specs=(
            P("dp", "seq", None),
            P("dp"),
            P(),
            P(),
            P(),
            P(),
            P(),
            P(),
            P(),
            P(),
            P(),
            P(),
            P(),
            P(),
            P(),
            P(),
            P(),
            P("dp", "seq", None),
        ),
        out_specs=(
            P("dp", "seq", None),
            P("dp", "seq", None),
            P(),
            P(),
            P("dp", None),
            P(),
            P("dp", None),
            P("dp", None),
            P(),
            P("dp", None),
            P(),
            P(),
            P(),
            P("dp", None),
            P(),
            P("dp", None),
            P(),
            P(),
            P(),
            P(),
        ),
        check_vma=False,
    )
```

profile of v0, /device:TPU:0, one launch (start us, length us, event | category | flops | bytes accessed | tf_op | source)
XLA Modules:
  0.0 1405.2 jit_solution(11405120334731023091)
XLA Ops:
  29.3 9.3 all-to-all-done
  53.6 9.4 all-to-all-done.1
  96.7 136.2 %while.34 = (s32[]{:T(128)}, bf16[2,2048,3,64]{1,3,2,0:T(8,128)(2,1)}, f32[2,3,2048]{2,1,0:T(4,128)S(1)}, bf16[2,2048,3,64]{1,3,2,0:T(8,128)(2,1)}, bf16[2,2048,...) while((s32[]{:T(128)}, ...), condition=%wide.region_5.6_spmd.clone, body=%wide.region_2.5_spmd.clone.sunk | while | flops 1680016384 | bytes 85852360 | solution.py:109
  96.8 11.2 fusion.141
  108.0 11.2 exponential_reduce_fusion.2
  119.2 11.5 fusion.142
  130.8 11.2 fusion.141
  142.0 11.2 exponential_reduce_fusion.2
  153.3 11.5 fusion.142
  164.9 11.2 fusion.141
  176.1 11.2 exponential_reduce_fusion.2
  187.3 11.5 fusion.142
  198.9 11.2 fusion.141
  210.1 11.2 exponential_reduce_fusion.2
  221.4 11.5 fusion.142
  247.4 22.1 %all-to-all-done.3 = bf16[2,2048,1,192]{3,0,2,1:T(2,128)(2,1)} async-done(((bf16[2,2048,1,192]{3,0,2,1:T(2,128)(2,1)}), bf16[2,2048,1,192]{3,0,2,1:T(2,128)(2,1)}, u32[]{:S(2)}, u32[]{:S(2)}) %all-to-all-start.3) | async-done | bytes 1572896 | tf_op jit(solution)/shard_map/all_to_all | solution.py:110
  281.5 35.4 %multiply_convert_fusion.1 = (bf16[1024,3072]{1,0:T(8,128)(2,1)}, f32[1024,3072]{1,0:T(8,128)}, f32[1024,3072]{1,0:T(8,128)}) fusion(f32[3072]{0:T(1024)S(1)} %copy-done.67, bf16[768,3072]{1,0:T(8,128)(2,1)S(1)} %bitcast.230, f32[1024,768]{1,0:T(8,128)S(1)} %get-tuple-element.448, f32[768]{0:T(1024)S(1)} %copy-done.45, f32[768]{0:T(1024)S(1)} %copy-done.39, ...), kind=kOutput, calls=%fused_computation.49 | convolution fusion | flops 5043388416 | bytes 39348224 | tf_op jit(solution)/shard_map/dot_general | solution.py:117
  316.9 17.4 %convert_reduce_fusion = (f32[3072]{0:T(1024)}, bf16[1024,3072]{1,0:T(8,128)(2,1)}) fusion(f32[1024,3072]{1,0:T(8,128)} %get-tuple-element.446, bf16[1024,768]{1,0:T(8,128)(2,1)S(1)} %copy-done.18, bf16[3072,768]{1,0:T(8,128)(2,1)} %param.37, f32[1024,3072]{1,0:T(8,128)} %get-tuple-element.461, f32[3072]{0:T(1024)S(1)} %copy-done.67), kind=kOutput, calls=%fused_computation.47 | convolution fusion | flops 4885312512 | bytes 37773312 | tf_op jit(solution)/shard_map/td,fd->tf/dot_general | solution.py:129
  343.6 11.0 fusion.43
  375.1 15.2 %all-to-all-done.4 = bf16[2,512,4,192]{1,0,3,2:T(2,128)(2,1)} async-done(((bf16[2,512,4,192]{1,0,3,2:T(2,128)(2,1)}), bf16[2,512,4,192]{1,0,3,2:T(2,128)(2,1)}, u32[]{:S(2)}, u32[]{:S(2)}) %all-to-all-start.4) | async-done | bytes 1572896 | tf_op jit(solution)/shard_map/all_to_all | solution.py:150
  399.3 330.1 %while.35 = (s32[]{:T(128)}, bf16[2,2048,3,64]{1,3,2,0:T(8,128)(2,1)}, f32[2,2048,3,64]{1,3,2,0:T(8,128)}, f32[2,2048,3,64]{1,3,2,0:T(8,128)}, bf16[2,2048,3,64]...) while((s32[]{:T(128)}, ...), condition=%wide.region_12.13_spmd.clone, body=%wide.region_10.0_spmd.clone.sunk | while | flops 4125230080 | bytes 208113888 | solution.py:186
  399.5 11.2 fusion.152
  411.4 17.1 %multiply_reduce_fusion.6 = (f32[2,3,512]{2,1,0:T(4,128)S(1)}, f32[2,3,512,2048]{3,2,1,0:T(8,128)}) fusion(f32[2,3,512,2048]{3,2,1,0:T(8,128)} %fusion.152, f32[2,3,512]{2,1,0:T(4,128)S(1)} %constant_dynamic-slice_fusion.2, pred[2,2048]{1,0:T(4,128)(4,1)S(1)} %iota_compare_fusion.5, bf16[2,2048,3,64]{1,3,2,0:T(8,128)(2,1)} %get-tuple-element.650, ...), kind=kOutput, calls=%fused_computation.20.clone.1 | convolution fusion | flops 836760576 | bytes 52326404 | tf_op jit(solution)/shard_map/while/body/eval_jaxpr/sqhd,skhd->shqk/dot_general | solution.py:162
  428.6 21.4 %multiply_convert_fusion.4 = bf16[2,3,512,2048]{3,2,1,0:T(8,128)(2,1)} fusion(f32[2,3,512,2048]{3,2,1,0:T(8,128)} %get-tuple-element.579, f32[2,3,512,2048]{3,2,1,0:T(8,128)} %fusion.152, f32[2,3,512]{2,1,0:T(4,128)S(1)} %get-tuple-element.580, f32[2,3,512]{2,1,0:T(4,128)S(1)} %constant_dynamic-slice_fusion.2, pred[2,2048]{1,0:T(4,128)(4,1)S(1)} %iota_compare_fusion.5), kind=kLoop, calls=%fused_computation.19.clone.1 | loop fusion | flops 37748736 | bytes 62943232 | tf_op jit(solution)/shard_map/while/body/eval_jaxpr/convert_element_type | solution.py:166
  458.7 9.3 fusion.153
  467.9 12.3 bitcast_add_fusion.7
  480.2 11.2 fusion.152
  492.2 17.1 %multiply_reduce_fusion.6 = (f32[2,3,512]{2,1,0:T(4,128)S(1)}, f32[2,3,512,2048]{3,2,1,0:T(8,128)}) fusion(f32[2,3,512,2048]{3,2,1,0:T(8,128)} %fusion.152, f32[2,3,512]{2,1,0:T(4,128)S(1)} %constant_dynamic-slice_fusion.2, pred[2,2048]{1,0:T(4,128)(4,1)S(1)} %iota_compare_fusion.5, bf16[2,2048,3,64]{1,3,2,0:T(8,128)(2,1)} %get-tuple-element.650, ...), kind=kOutput, calls=%fused_computation.20.clone.1 | convolution fusion | flops 836760576 | bytes 52326404 | tf_op jit(solution)/shard_map/while/body/eval_jaxpr/sqhd,skhd->shqk/dot_general | solution.py:162
  509.3 21.4 %multiply_convert_fusion.4 = bf16[2,3,512,2048]{3,2,1,0:T(8,128)(2,1)} fusion(f32[2,3,512,2048]{3,2,1,0:T(8,128)} %get-tuple-element.579, f32[2,3,512,2048]{3,2,1,0:T(8,128)} %fusion.152, f32[2,3,512]{2,1,0:T(4,128)S(1)} %get-tuple-element.580, f32[2,3,512]{2,1,0:T(4,128)S(1)} %constant_dynamic-slice_fusion.2, pred[2,2048]{1,0:T(4,128)(4,1)S(1)} %iota_compare_fusion.5), kind=kLoop, calls=%fused_computation.19.clone.1 | loop fusion | flops 37748736 | bytes 62943232 | tf_op jit(solution)/shard_map/while/body/eval_jaxpr/convert_element_type | solution.py:166
  530.7 9.6 bitcast_add_fusion.6
  540.3 9.3 fusion.153
  549.6 13.7 bitcast_add_fusion.7
  563.3 11.2 fusion.152
  575.3 17.1 %multiply_reduce_fusion.6 = (f32[2,3,512]{2,1,0:T(4,128)S(1)}, f32[2,3,512,2048]{3,2,1,0:T(8,128)}) fusion(f32[2,3,512,2048]{3,2,1,0:T(8,128)} %fusion.152, f32[2,3,512]{2,1,0:T(4,128)S(1)} %constant_dynamic-slice_fusion.2, pred[2,2048]{1,0:T(4,128)(4,1)S(1)} %iota_compare_fusion.5, bf16[2,2048,3,64]{1,3,2,0:T(8,128)(2,1)} %get-tuple-element.650, ...), kind=kOutput, calls=%fused_computation.20.clone.1 | convolution fusion | flops 836760576 | bytes 52326404 | tf_op jit(solution)/shard_map/while/body/eval_jaxpr/sqhd,skhd->shqk/dot_general | solution.py:162
  592.4 21.4 %multiply_convert_fusion.4 = bf16[2,3,512,2048]{3,2,1,0:T(8,128)(2,1)} fusion(f32[2,3,512,2048]{3,2,1,0:T(8,128)} %get-tuple-element.579, f32[2,3,512,2048]{3,2,1,0:T(8,128)} %fusion.152, f32[2,3,512]{2,1,0:T(4,128)S(1)} %get-tuple-element.580, f32[2,3,512]{2,1,0:T(4,128)S(1)} %constant_dynamic-slice_fusion.2, pred[2,2048]{1,0:T(4,128)(4,1)S(1)} %iota_compare_fusion.5), kind=kLoop, calls=%fused_computation.19.clone.1 | loop fusion | flops 37748736 | bytes 62943232 | tf_op jit(solution)/shard_map/while/body/eval_jaxpr/convert_element_type | solution.py:166
  613.8 9.6 bitcast_add_fusion.6
  623.4 9.3 fusion.153
  632.7 13.5 bitcast_add_fusion.7
  646.2 11.2 fusion.152
  658.2 17.1 %multiply_reduce_fusion.6 = (f32[2,3,512]{2,1,0:T(4,128)S(1)}, f32[2,3,512,2048]{3,2,1,0:T(8,128)}) fusion(f32[2,3,512,2048]{3,2,1,0:T(8,128)} %fusion.152, f32[2,3,512]{2,1,0:T(4,128)S(1)} %constant_dynamic-slice_fusion.2, pred[2,2048]{1,0:T(4,128)(4,1)S(1)} %iota_compare_fusion.5, bf16[2,2048,3,64]{1,3,2,0:T(8,128)(2,1)} %get-tuple-element.650, ...), kind=kOutput, calls=%fused_computation.20.clone.1 | convolution fusion | flops 836760576 | bytes 52326404 | tf_op jit(solution)/shard_map/while/body/eval_jaxpr/sqhd,skhd->shqk/dot_general | solution.py:162
  675.3 21.4 %multiply_convert_fusion.4 = bf16[2,3,512,2048]{3,2,1,0:T(8,128)(2,1)} fusion(f32[2,3,512,2048]{3,2,1,0:T(8,128)} %get-tuple-element.579, f32[2,3,512,2048]{3,2,1,0:T(8,128)} %fusion.152, f32[2,3,512]{2,1,0:T(4,128)S(1)} %get-tuple-element.580, f32[2,3,512]{2,1,0:T(4,128)S(1)} %constant_dynamic-slice_fusion.2, pred[2,2048]{1,0:T(4,128)(4,1)S(1)} %iota_compare_fusion.5), kind=kLoop, calls=%fused_computation.19.clone.1 | loop fusion | flops 37748736 | bytes 62943232 | tf_op jit(solution)/shard_map/while/body/eval_jaxpr/convert_element_type | solution.py:166
  696.6 9.6 bitcast_add_fusion.6
  706.3 9.3 fusion.153
  715.5 13.7 bitcast_add_fusion.7
  739.0 9.9 fusion.82
  755.0 9.6 all-to-all-done.6
  790.5 10.7 reshape.391
  885.0 461.3 %all-reduce.8 = (f32[768]{0:T(1024)}, f32[768]{0:T(1024)}, bf16[589824]{0:T(1024)(128)(2,1)}, f32[768]{0:T(1024)}, bf16[589824]{0:T(1024)(128)(2,1)}, /*index=5*...) all-reduce(f32[768]{0:T(1024)S(1)} %get-tuple-element.376, ...), channel_id=1, replica_groups=mesh['dp'=8,'seq'=4] {'dp','seq'}, use_global_device_ids=true, to_apply=%region_16.17 | all-reduce | flops 7087108 | bytes 42541088 | tf_op jit(solution)/shard_map/psum | solution.py:229
  (295 shorter events, 332.0 us)
Async XLA Ops:
  0.7 276.7 %copy-start = (bf16[768,768]{1,0:T(8,128)(2,1)S(1)}, bf16[768,768]{1,0:T(8,128)(2,1)}, u32[]{:S(2)}) copy-start(bf16[768,768]{1,0:T(8,128)(2,1)} %param.31) | copy-start | bytes 3538948
  0.7 5.1 copy-start.4
  0.7 5.1 copy-start.32
  0.7 5.1 copy-start.55
  0.7 6.9 copy-start.65
  0.7 6.9 copy-start.68
  14.3 24.3 %all-to-all-start = ((bf16[2,512,4,192]{1,0,3,2:T(2,128)(2,1)}), bf16[2,512,4,192]{1,0,3,2:T(2,128)(2,1)S(1)}, u32[]{:S(2)}, u32[]{:S(2)}) async-start(bf16[2,512,4,192]{1,0,3,2:T(2,128)(2,1)} %reshape.358), calls=%async_computation | async-start | bytes 3145728 | tf_op jit(solution)/shard_map/all_to_all | solution.py:76
  25.4 17.5 %copy-start.69 = (f32[768]{0:T(1024)S(1)}, f32[768]{0:T(1024)}, u32[]{:S(2)}) copy-start(f32[768]{0:T(1024)} %param.30) | copy-start | bytes 9220
  38.6 24.5 %all-to-all-start.1 = ((bf16[2,512,4,192]{1,0,3,2:T(2,128)(2,1)}), bf16[2,512,4,192]{1,0,3,2:T(2,128)(2,1)}, u32[]{:S(2)}, u32[]{:S(2)}) async-start(bf16[2,512,4,192]{1,0,3,2:T(2,128)(2,1)} %reshape.360), calls=%async_computation.1 | async-start | bytes 3145728 | tf_op jit(solution)/shard_map/all_to_all | solution.py:77
  63.1 24.6 %all-to-all-start.2 = ((bf16[2,512,4,192]{1,0,3,2:T(2,128)(2,1)}), bf16[2,512,4,192]{1,0,3,2:T(2,128)(2,1)}, u32[]{:S(2)}, u32[]{:S(2)}) async-start(bf16[2,512,4,192]{1,0,3,2:T(2,128)(2,1)} %reshape.362), calls=%async_computation.2 | async-start | bytes 3145728 | tf_op jit(solution)/shard_map/all_to_all | solution.py:78
  91.5 5.2 copy-start.37
  108.0 11.2 copy-start.8
  142.0 11.2 copy-start.8
  176.1 11.2 copy-start.8
  210.1 11.2 copy-start.8
  232.9 6.3 copy-start.2
  232.9 6.3 copy-start.29
  239.2 30.4 %all-to-all-start.3 = ((bf16[2,2048,1,192]{3,0,2,1:T(2,128)(2,1)}), bf16[2,2048,1,192]{3,0,2,1:T(2,128)(2,1)}, u32[]{:S(2)}, u32[]{:S(2)}) async-start(bf16[2,2048,1,192]{3,0,2,1:T(2,128)(2,1)} %copy.84), calls=%async_computation.3 | async-start | bytes 4194304 | tf_op jit(solution)/shard_map/all_to_all | solution.py:110
  244.5 111.6 %copy-start.43 = (f32[1,4,2,128]{3,1,2,0:T(4,128)}, f32[1,4,2,128]{3,1,2,0:T(4,128)S(1)}, u32[]{:S(2)}) copy-start(f32[1,4,2,128]{3,1,2,0:T(4,128)S(1)} %copy.104) | copy-start | bytes 12292
  280.7 73.9 %copy-start.9 = (f32[1024,768]{1,0:T(8,128)}, f32[1024,768]{1,0:T(8,128)S(1)}, u32[]{:S(2)}) copy-start(f32[1024,768]{1,0:T(8,128)S(1)} %get-tuple-element.448) | copy-start | bytes 9437188
  280.7 73.9 %copy-start.27 = (f32[1024]{0:T(1024)}, f32[1024]{0:T(1024)S(1)}, u32[]{:S(2)}) copy-start(f32[1024]{0:T(1024)S(1)} %broadcast_multiply_fusion) | copy-start | bytes 12292
  281.5 73.1 %copy-start.30 = (f32[1024]{0:T(1024)}, f32[1024]{0:T(1024)S(1)}, u32[]{:S(2)}) copy-start(f32[1024]{0:T(1024)S(1)} %fusion.62) | copy-start | bytes 12292
  281.5 35.4 %copy-start.18 = (bf16[1024,768]{1,0:T(8,128)(2,1)S(1)}, bf16[1024,768]{1,0:T(8,128)(2,1)}, u32[]{:S(2)}) copy-start(bf16[1024,768]{1,0:T(8,128)(2,1)} %fusion.59) | copy-start | bytes 4718596
  334.3 9.3 copy-start.70
  334.3 9.3 copy-start.72
  334.3 9.3 copy-start.73
  363.3 6.9 copy-start.38
  363.3 6.9 copy-start.54
  363.3 7.6 copy-start.59
  365.6 7.6 copy-start.6
  365.6 7.6 copy-start.33
  365.6 7.6 copy-start.48
  365.6 7.6 copy-start.56
  365.7 7.6 copy-start.58
  365.7 24.6 %all-to-all-start.4 = ((bf16[2,512,4,192]{1,0,3,2:T(2,128)(2,1)}), bf16[2,512,4,192]{1,0,3,2:T(2,128)(2,1)}, u32[]{:S(2)}, u32[]{:S(2)}) async-start(bf16[2,512,4,192]{1,0,3,2:T(2,128)(2,1)} %reshape.367), calls=%async_computation.4 | async-start | bytes 3145728 | tf_op jit(solution)/shard_map/all_to_all | solution.py:150
  394.0 5.3 copy-start.3
  735.4 29.2 %all-to-all-start.6 = ((bf16[2,2048,1,192]{3,0,2,1:T(2,128)(2,1)}), bf16[2,2048,1,192]{3,0,2,1:T(2,128)(2,1)S(1)}, u32[]{:S(2)}, u32[]{:S(2)}) async-start(bf16[2,2048,1,192]{3,0,2,1:T(2,128)(2,1)} %copy.92), calls=%async_computation.6 | async-start | bytes 4194304 | tf_op jit(solution)/shard_map/all_to_all | solution.py:193
  748.9 20.7 %copy-start.28 = (f32[1024]{0:T(1024)S(1)}, f32[1024]{0:T(1024)}, u32[]{:S(2)}) copy-start(f32[1024]{0:T(1024)} %copy-done.27) | copy-start | bytes 12292
  748.9 20.7 %copy-start.31 = (f32[1024]{0:T(1024)S(1)}, f32[1024]{0:T(1024)}, u32[]{:S(2)}) copy-start(f32[1024]{0:T(1024)} %copy-done.30) | copy-start | bytes 12292
  748.9 20.7 %copy-start.40 = (f32[768]{0:T(1024)S(1)}, f32[768]{0:T(1024)}, u32[]{:S(2)}) copy-start(f32[768]{0:T(1024)} %param.33) | copy-start | bytes 9220
  748.9 20.7 %copy-start.46 = (f32[768]{0:T(1024)S(1)}, f32[768]{0:T(1024)}, u32[]{:S(2)}) copy-start(f32[768]{0:T(1024)} %param.34) | copy-start | bytes 9220
  766.0 58.8 %all-to-all-start.5 = ((bf16[2,2048,1,192]{3,0,2,1:T(2,128)(2,1)}), bf16[2,2048,1,192]{3,0,2,1:T(2,128)(2,1)S(1)}, u32[]{:S(2)}, u32[]{:S(2)}) async-start(bf16[2,2048,1,192]{3,0,2,1:T(2,128)(2,1)} %copy.89), calls=%async_computation.5 | async-start | bytes 4194304 | tf_op jit(solution)/shard_map/all_to_all | solution.py:190
  778.6 5.9 copy-start.17
  778.6 5.9 copy-start.25
  824.8 30.6 %all-to-all-start.7 = ((bf16[2,2048,1,192]{3,0,2,1:T(2,128)(2,1)}), bf16[2,2048,1,192]{3,0,2,1:T(2,128)(2,1)}, u32[]{:S(2)}, u32[]{:S(2)}) async-start(bf16[2,2048,1,192]{3,0,2,1:T(2,128)(2,1)} %copy.95), calls=%async_computation.7 | async-start | bytes 4194304 | tf_op jit(solution)/shard_map/all_to_all | solution.py:200
  1358.2 38.3 %copy-start.44 = (f32[1,4,2,128]{3,1,2,0:T(4,128)S(1)}, f32[1,4,2,128]{3,1,2,0:T(4,128)}, u32[]{:S(2)}) copy-start(f32[1,4,2,128]{3,1,2,0:T(4,128)} %copy-done.43) | copy-start | bytes 12292
  1358.2 38.3 %copy-start.52 = (f32[1024]{0:T(1024)S(1)}, f32[1024]{0:T(1024)}, u32[]{:S(2)}) copy-start(f32[1024]{0:T(1024)} %copy-done.51) | copy-start | bytes 12292
  1396.5 5.1 copy-start.1
  (39 other events, 100.0 us)
where the time goes:
time: 1420 us; the launch traced here: 1410 us
  blocking collectives  498 us (35%)
  matrix products  462 us (33%)
  other arithmetic  163 us (11%)
  local copies, waits for them, and re-layouts  158 us (11%)
  waiting for transfers between devices  81.3 us (6%)
  starting transfers between devices  34.3 us (2%)
    psum x1, blocking collectives, local(): lax.psum((jnp.sum(stream * stream), jnp.sum(keep_rows * branch_attn * bra...  461 us
    dot_general x8, matrix products, scores_of(): jnp.einsum('sqhd,skhd->shqk', query_blk, head_k, preferred_element_type=j...  89.6 us
    convert_element_type x4, other arithmetic, backward_block(): grad_scores = (probability * (grad_prob - row_sums)).astype(jnp.bfloat16)  85.4 us
    dot_general x4, matrix products, backward_block(): jnp.einsum('sqhd,skhd->shqk', grad_out_blk, head_v, preferred_element_typ...  68.4 us
    dot_general x4, matrix products, backward_block(): jnp.einsum('shqk,sqhd->skhd', probability_low, grad_out_blk, preferred_el...  53.2 us
    dot_general x4, matrix products, forward_block(): jnp.einsum('shqk,skhd->sqhd', probability_low, head_v, preferred_element_...  45.9 us
    reduce_sum x4, other arithmetic, forward_block(): row_total = jnp.sum(jnp.exp(logits - row_max), axis=-1, keepdims=True)  44.8 us
    dot_general x4, matrix products, backward_block(): jnp.einsum('shqk,sqhd->skhd', grad_scores, query_blk, preferred_element_t...  37.6 us
  transfers between devices with their start and end apart: 8, of which 7 were waited for; matrix products, arithmetic and copies ran while one was open for 9% of the time, Pallas kernels for 0%

commit v1 on v0

v1 whole, which is shorter than its diff:
```python
import functools

import jax
import jax.numpy as jnp
from jax import lax
from jax.experimental import pallas as pl
from jax.experimental.pallas import tpu as pltpu
from jax.sharding import PartitionSpec as P

HEADS = 12
HEAD_DIM = 64
EPSILON = 1e-12
NEGATIVE = -1e30
PAIR = 2 * HEAD_DIM
NT = ((1,), (1,))
NN = ((1,), (0,))
TN = ((0,), (0,))


def norm_apply(values, gain_vec, shift_vec):
    average = jnp.mean(values, axis=-1, keepdims=True)
    centered = values - average
    spread = jnp.mean(centered * centered, axis=-1, keepdims=True)
    return centered * lax.rsqrt(spread + EPSILON) * gain_vec + shift_vec


def exact_gelu(values):
    return jax.nn.gelu(values, approximate=False)


def dot(left, right, dims):
    return lax.dot_general(left, right, (dims, ((), ())), preferred_element_type=jnp.float32)


def key_valid(info_ref, keys_total):
    spots = lax.broadcasted_iota(jnp.int32, (keys_total, 1), 0)
    blocks = info_ref.shape[0] - 1
    block_len = keys_total // blocks
    places = spots
    for index in range(blocks):
        inside = (spots >= index * block_len) & (spots < (index + 1) * block_len)
        places = jnp.where(inside, spots - index * block_len + info_ref[index + 1], places)
    return places < info_ref[0]


def attend_body(info_ref, q_ref, k_ref, v_ref, out_ref, lse_ref):
    lane = lax.broadcasted_iota(jnp.int32, (1, PAIR), 1)
    scale = jnp.bfloat16(HEAD_DIM ** (-0.5))
    queries = q_ref[...] * scale
    keys = k_ref[...]
    values_t = v_ref[...].T
    valid = key_valid(info_ref, keys.shape[0])
    outs = []
    for head in range(2):
        mine = (lane < HEAD_DIM) if head == 0 else (lane >= HEAD_DIM)
        scores = dot(keys, jnp.where(mine, queries, jnp.zeros_like(queries)), NT)
        scores = jnp.where(valid, scores, NEGATIVE)
        top = jnp.max(scores, axis=0, keepdims=True)
        weights = jnp.exp(scores - top)
        total = jnp.sum(weights, axis=0, keepdims=True)
        mixed = dot(
            values_t[HEAD_DIM * head : HEAD_DIM * (head + 1)], weights.astype(jnp.bfloat16), NN
        )
        outs.append(mixed * (1.0 / total))
        lse_ref[0, head : head + 1, :] = top + jnp.log(total)
    out_ref[...] = jnp.concatenate(outs, axis=0).T.astype(jnp.bfloat16)


def attend(info, queries, keys, values, block):
    tokens, width = queries.shape
    total = keys.shape[0]
    pairs = width // PAIR
    q_spec = pl.BlockSpec((block, PAIR), lambda h, i, n: (i, h))
    k_spec = pl.BlockSpec((total, PAIR), lambda h, i, n: (0, h))
    return pl.pallas_call(
        attend_body,
        grid_spec=pltpu.PrefetchScalarGridSpec(
            num_scalar_prefetch=1,
            grid=(pairs, tokens // block),
            in_specs=[q_spec, k_spec, k_spec],
            out_specs=[q_spec, pl.BlockSpec((1, 2, block), lambda h, i, n: (h, 0, i))],
        ),
        out_shape=[
            jax.ShapeDtypeStruct((tokens, width), jnp.bfloat16),
            jax.ShapeDtypeStruct((pairs, 2, tokens), jnp.float32),
        ],
        compiler_params=pltpu.CompilerParams(vmem_limit_bytes=48 << 20),
        cost_estimate=pl.CostEstimate(
            flops=16 * tokens * total * width, bytes_accessed=1 << 23, transcendentals=0
        ),
        name="attend",
    )(info, queries, keys, values)


def attend_back_body(
    info_ref, q_ref, k_ref, v_ref, do_ref, o_ref, lse_ref, dq_ref, dk_ref, dv_ref, dk_acc, dv_acc
):
    step = pl.program_id(1)
    lane = lax.broadcasted_iota(jnp.int32, (1, PAIR), 1)
    scale = jnp.bfloat16(HEAD_DIM ** (-0.5))
    grad_out = do_ref[...]
    queries = q_ref[...] * scale
    keys = k_ref[...]
    values = v_ref[...]
    product = grad_out.astype(jnp.float32) * o_ref[...].astype(jnp.float32)
    pick = (
        lax.broadcasted_iota(jnp.int32, (8, PAIR), 1) // HEAD_DIM
        == lax.broadcasted_iota(jnp.int32, (8, PAIR), 0)
    ).astype(jnp.float32)
    row_sums = lax.dot_general(
        pick,
        product,
        (NT, ((), ())),
        precision=lax.Precision.HIGHEST,
        preferred_element_type=jnp.float32,
    )
    valid = key_valid(info_ref, keys.shape[0])
    zero = jnp.zeros_like(queries)
    grad_k = 0
    grad_v = 0
    grad_q = 0
    for head in range(2):
        mine = (lane < HEAD_DIM) if head == 0 else (lane >= HEAD_DIM)
        query_h = jnp.where(mine, queries, zero)
        out_h = jnp.where(mine, grad_out, zero)
        scores = jnp.where(valid, dot(keys, query_h, NT), NEGATIVE)
        weights = jnp.exp(scores - lse_ref[0, head : head + 1, :])
        grad_w = dot(values, out_h, NT)
        grad_s = (weights * (grad_w - row_sums[head : head + 1])).astype(jnp.bfloat16)
        grad_v = grad_v + dot(weights.astype(jnp.bfloat16), out_h, NN)
        grad_k = grad_k + dot(grad_s, query_h, NN)
        grad_q_h = dot(grad_s, keys, TN)
        grad_q = grad_q_h if head == 0 else jnp.where(mine, grad_q_h, grad_q)
    dq_ref[...] = (grad_q * (HEAD_DIM ** (-0.5))).astype(jnp.bfloat16)

    @pl.when(step == 0)
    def _():
        dk_acc[...] = grad_k
        dv_acc[...] = grad_v

    @pl.when(step > 0)
    def _():
        dk_acc[...] += grad_k
        dv_acc[...] += grad_v

    @pl.when(step == pl.num_programs(1) - 1)
    def _():
        dk_ref[...] = dk_acc[...].astype(jnp.bfloat16)
        dv_ref[...] = dv_acc[...].astype(jnp.bfloat16)


def attend_back(info, queries, keys, values, grad_out, out, log_sums, block):
    tokens, width = queries.shape
    total = keys.shape[0]
    pairs = width // PAIR
    q_spec = pl.BlockSpec((block, PAIR), lambda h, i, n: (i, h))
    k_spec = pl.BlockSpec((total, PAIR), lambda h, i, n: (0, h))
    return pl.pallas_call(
        attend_back_body,
        grid_spec=pltpu.PrefetchScalarGridSpec(
            num_scalar_prefetch=1,
            grid=(pairs, tokens // block),
            in_specs=[
                q_spec,
                k_spec,
                k_spec,
                q_spec,
                q_spec,
                pl.BlockSpec((1, 2, block), lambda h, i, n: (h, 0, i)),
            ],
            out_specs=[q_spec, k_spec, k_spec],
            scratch_shapes=[pltpu.VMEM((total, PAIR), jnp.float32)] * 2,
        ),
        out_shape=[
            jax.ShapeDtypeStruct((tokens, width), jnp.bfloat16),
            jax.ShapeDtypeStruct((total, width), jnp.bfloat16),
            jax.ShapeDtypeStruct((total, width), jnp.bfloat16),
        ],
        compiler_params=pltpu.CompilerParams(vmem_limit_bytes=48 << 20),
        cost_estimate=pl.CostEstimate(
            flops=40 * tokens * total * width, bytes_accessed=1 << 24, transcendentals=0
        ),
        name="attend_back",
    )(info, queries, keys, values, grad_out, out, log_sums)


def local(
    inputs,
    lengths,
    first_gain,
    first_shift,
    query_weight,
    query_bias,
    key_weight,
    value_weight,
    value_bias,
    output_weight,
    output_bias,
    second_gain,
    second_shift,
    inner_weight,
    inner_bias,
    outer_weight,
    outer_bias,
    cotangent,
):
    groups = lax.axis_size("seq")
    seq_count, local_len, width = inputs.shape
    full_len = local_len * groups
    tokens_here = seq_count * local_len
    place = lax.axis_index("seq")
    half = groups // 2
    row = place // half
    across = [(i, (i + half) % groups) for i in range(groups)]
    beside = [(i, i ^ 1) for i in range(groups)]
    there = lax.rem(place + half, groups)
    near = place + 1 - 2 * lax.rem(place, 2)

    def mine_of(array):
        return lax.dynamic_index_in_dim(array, row, 0, keepdims=False)

    def swap(array):
        return lax.ppermute(
            lax.dynamic_index_in_dim(array, 1 - row, 0, keepdims=False), "seq", across
        )

    def give_back(array):
        own = array[:local_len]
        other = lax.ppermute(array[local_len:], "seq", across)
        return jnp.where(row == 0, jnp.stack([own, other]), jnp.stack([other, own]))

    length = lax.dynamic_index_in_dim(lengths, row, 0, keepdims=False)
    starts = jnp.stack(
        [place, there, near, lax.rem(near + half, groups)]
    ).astype(jnp.int32) * local_len
    info = jnp.concatenate([length[None], starts])
    spots = jnp.concatenate(
        [starts[0] + jnp.arange(local_len, dtype=jnp.int32), starts[1] + jnp.arange(local_len, dtype=jnp.int32)]
    )
    keep_rows = (spots < length).astype(jnp.float32)[:, None]
    own_in = mine_of(inputs)
    far_in = swap(inputs)
    cot = jnp.concatenate([mine_of(cotangent), swap(cotangent)], axis=0)

    def project(rows):
        normed = norm_apply(rows.astype(jnp.float32), first_gain, first_shift).astype(jnp.bfloat16)
        q = (
            jnp.dot(normed, query_weight, preferred_element_type=jnp.float32) + query_bias
        ).astype(jnp.bfloat16)
        k = jnp.dot(normed, key_weight, preferred_element_type=jnp.float32).astype(jnp.bfloat16)
        v = (
            jnp.dot(normed, value_weight, preferred_element_type=jnp.float32) + value_bias
        ).astype(jnp.bfloat16)
        return q, k, v

    parts = (project(own_in), project(far_in))
    queries = jnp.concatenate([parts[0][0], parts[1][0]], axis=0)

    def all_keys(index):
        sent = [lax.ppermute(part[index], "seq", beside) for part in parts]
        return jnp.concatenate([parts[0][index], parts[1][index], *sent], axis=0)

    keys = all_keys(1)
    values = all_keys(2)
    flat_in = jnp.concatenate([own_in, far_in], axis=0).astype(jnp.float32)
    normed_one, norm_one_back = jax.vjp(norm_apply, flat_in, first_gain, first_shift)
    normed_one_low = normed_one.astype(jnp.bfloat16)
    attended, log_sums = attend(info, queries, keys, values, 512)
    branch_attn = jnp.dot(attended, output_weight, preferred_element_type=jnp.float32) + output_bias
    hidden = flat_in + branch_attn
    normed_two, norm_two_back = jax.vjp(norm_apply, hidden, second_gain, second_shift)
    normed_two_low = normed_two.astype(jnp.bfloat16)
    inner = jnp.dot(normed_two_low, inner_weight, preferred_element_type=jnp.float32) + inner_bias
    activated_full, gelu_back = jax.vjp(exact_gelu, inner)
    activated = activated_full.astype(jnp.bfloat16)
    branch_ffn = jnp.dot(activated, outer_weight, preferred_element_type=jnp.float32) + outer_bias
    stream = keep_rows * (hidden + branch_ffn)
    result = give_back(stream.astype(jnp.bfloat16))
    grad_stream = keep_rows * cot.astype(jnp.float32)
    grad_ffn_low = grad_stream.astype(jnp.bfloat16)
    grad_outer_weight = jnp.einsum(
        "tf,td->fd", activated, grad_ffn_low, preferred_element_type=jnp.float32
    )
    grad_outer_bias = jnp.sum(grad_ffn_low, axis=0, dtype=jnp.float32)
    grad_activated = jnp.einsum(
        "td,fd->tf", grad_ffn_low, outer_weight, preferred_element_type=jnp.float32
    )
    grad_inner_low = gelu_back(grad_activated)[0].astype(jnp.bfloat16)
    grad_inner_weight = jnp.einsum(
        "td,tf->df", normed_two_low, grad_inner_low, preferred_element_type=jnp.float32
    )
    grad_inner_bias = jnp.sum(grad_inner_low, axis=0, dtype=jnp.float32)
    grad_normed_two = jnp.einsum(
        "tf,df->td", grad_inner_low, inner_weight, preferred_element_type=jnp.float32
    )
    grad_hidden_norm, grad_second_gain, grad_second_shift = norm_two_back(grad_normed_two)
    grad_hidden = grad_stream + grad_hidden_norm
    grad_attn_low = grad_hidden.astype(jnp.bfloat16)
    grad_output_weight = jnp.einsum(
        "tc,td->cd", attended, grad_attn_low, preferred_element_type=jnp.float32
    )
    grad_output_bias = jnp.sum(grad_attn_low, axis=0, dtype=jnp.float32)
    grad_attended = jnp.einsum(
        "td,cd->tc", grad_attn_low, output_weight, preferred_element_type=jnp.float32
    ).astype(jnp.bfloat16)
    grad_q_tok, grad_k_part, grad_v_part = attend_back(
        info, queries, keys, values, grad_attended, attended, log_sums, 256
    )

    def join(partial):
        far = lax.ppermute(partial[tokens_here:], "seq", beside)
        return (partial[:tokens_here].astype(jnp.float32) + far.astype(jnp.float32)).astype(
            jnp.bfloat16
        )

    grad_k_tok = join(grad_k_part)
    grad_v_tok = join(grad_v_part)
    grad_query_weight = jnp.einsum(
        "td,te->de", normed_one_low, grad_q_tok, preferred_element_type=jnp.float32
    )
    grad_key_weight = jnp.einsum(
        "td,te->de", normed_one_low, grad_k_tok, preferred_element_type=jnp.float32
    )
    grad_value_weight = jnp.einsum(
        "td,te->de", normed_one_low, grad_v_tok, preferred_element_type=jnp.float32
    )
    grad_query_bias = jnp.sum(grad_q_tok, axis=0, dtype=jnp.float32)
    grad_value_bias = jnp.sum(grad_v_tok, axis=0, dtype=jnp.float32)
    grad_normed_one = (
        jnp.einsum("te,de->td", grad_q_tok, query_weight, preferred_element_type=jnp.float32)
        + jnp.einsum("te,de->td", grad_k_tok, key_weight, preferred_element_type=jnp.float32)
        + jnp.einsum("te,de->td", grad_v_tok, value_weight, preferred_element_type=jnp.float32)
    )
    grad_in_norm, grad_first_gain, grad_first_shift = norm_one_back(grad_normed_one)
    grad_inputs = give_back((grad_hidden + grad_in_norm).astype(jnp.bfloat16))
    totals = lax.psum(
        (
            jnp.sum(stream * stream),
            jnp.sum(keep_rows * branch_attn * branch_attn),
            jnp.sum(keep_rows * branch_ffn * branch_ffn),
            jnp.sum(keep_rows),
            grad_first_gain,
            grad_first_shift,
            grad_query_bias,
            grad_value_bias,
            grad_output_bias,
            grad_second_gain,
            grad_second_shift,
            grad_inner_bias,
            grad_outer_bias,
        ),
        ("dp", "seq"),
    )
    denominator = totals[3] * width
    stream_scale = jnp.sqrt(totals[0] / denominator)
    attention_scale = jnp.sqrt(totals[1] / denominator)
    feedforward_scale = jnp.sqrt(totals[2] / denominator)
    data_groups = lax.axis_size("dp")

    def reduced(partial):
        piece = lax.psum_scatter(
            partial.astype(jnp.bfloat16), ("dp", "seq"), scatter_dimension=0, tiled=True
        )
        return lax.all_gather(piece, "seq", axis=0, tiled=True).astype(jnp.float32)

    summed_query = reduced(grad_query_weight)
    summed_key = reduced(grad_key_weight)
    summed_value = reduced(grad_value_weight)
    summed_output = reduced(grad_output_weight)
    summed_inner = reduced(grad_inner_weight)
    summed_outer = reduced(grad_outer_weight)
    return (
        result,
        grad_inputs,
        totals[4],
        totals[5],
        summed_query,
        totals[6],
        summed_key,
        summed_value,
        totals[7],
        summed_output,
        totals[8],
        totals[9],
        totals[10],
        summed_inner,
        totals[11],
        summed_outer,
        totals[12],
        stream_scale,
        attention_scale,
        feedforward_scale,
    )


def solution(mesh):
    return jax.shard_map(
        local,
        mesh=mesh,
        in_specs=(
            P("dp", "seq", None),
            P("dp"),
            P(),
            P(),
            P(),
            P(),
            P(),
            P(),
            P(),
            P(),
            P(),
            P(),
            P(),
            P(),
            P(),
            P(),
            P(),
            P("dp", "seq", None),
        ),
        out_specs=(
            P("dp", "seq", None),
            P("dp", "seq", None),
            P(),
            P(),
            P("dp", None),
            P(),
            P("dp", None),
            P("dp", None),
            P(),
            P("dp", None),
            P(),
            P(),
            P(),
            P("dp", None),
            P(),
            P("dp", None),
            P(),
            P(),
            P(),
            P(),
        ),
        check_vma=False,
    )
```

time: 1420 us -> 937 us (0.66)
  blocking collectives: 498 us -> 79.6 us
  waiting for transfers between devices: 81.3 us -> 490 us
  matrix products: 462 us -> 144 us
  local copies, waits for them, and re-layouts: 158 us -> 24.2 us
  Pallas kernels: 0 us -> 132 us
  other arithmetic: 163 us -> 31.9 us
  starting transfers between devices: 34.3 us -> 7.61 us
    reduce_scatter x0 -> x6, waiting for transfers between devices: none -> 472 us  [reduced(): lax.psum_scatter(partial.astype(jnp.bfloat16), ('dp', 'seq'), scatter_dim...]
    psum x1, blocking collectives: 461 us -> 41.7 us  [local(): lax.psum((jnp.sum(stream * stream), jnp.sum(keep_rows * branch_attn * bra...]
    dot_general x31 -> x6, matrix products: 343 us -> 15.3 us  [the longest x2 5.84 us: project(): jnp.dot(normed, query_weight, preferred_element_type=jnp.float32)]
    pallas_call x0 -> x2, Pallas kernels: none -> 132 us  [the longest x1 84 us: attend_back(): pl.pallas_call(attend_back_body, grid_spec=pltpu.PrefetchScalarGridSpec(n...]
    convert_element_type x11 -> x8, other arithmetic: 102 us -> 8.73 us  [the longest x6 5.14 us: reduced(): return lax.all_gather(piece, 'seq', axis=0, tiled=True).astype(jnp.float32)]
    all_to_all x8 -> x0, waiting for transfers between devices: 81.3 us -> none  [the longest x1 22.1 us: local(): lax.all_to_all(head_out.reshape(merged_shape), 'seq', split_axis=1, conca...]
    reshape x23 -> x0, local copies, waits for them, and re-layouts: 78.9 us -> none  [the longest x4 12.4 us: to_heads(): return flat.reshape(seq_count, local_len, groups, model_width // groups)]
    reduce_sum x5 -> x0, other arithmetic: 47.2 us -> none  [the longest x4 44.8 us: forward_block(): row_total = jnp.sum(jnp.exp(logits - row_max), axis=-1, keepdims=True)]
  transfers between devices with their start and end apart: 8 -> 16, of which waited for: 7 -> 8; matrix products, arithmetic and copies ran while one was open for 9% -> 15% of each run, Pallas kernels for 0% -> 5%
where the time goes in v1:
time: 937 us; the launch traced here: 930 us
  waiting for transfers between devices  490 us (52%)
  matrix products  144 us (15%)
  Pallas kernels  132 us (14%)
  blocking collectives  79.6 us (8%)
  other arithmetic  31.9 us (3%)
  local copies, waits for them, and re-layouts  24.2 us (3%)
  between operations  21.5 us (2%)
    reduce_scatter x6, waiting for transfers between devices, reduced(): lax.psum_scatter(partial.astype(jnp.bfloat16), ('dp', 'seq'), scatter_dim...  472 us
    pallas_call x1, Pallas kernels, attend_back(): pl.pallas_call(attend_back_body, grid_spec=pltpu.PrefetchScalarGridSpec(n...  84 us
    pallas_call x1, Pallas kernels, attend(): pl.pallas_call(attend_body, grid_spec=pltpu.PrefetchScalarGridSpec(num_sc...  47.7 us
    psum x1, blocking collectives, local(): lax.psum((jnp.sum(stream * stream), jnp.sum(keep_rows * branch_attn * bra...  41.7 us
    all_gather x6, blocking collectives, reduced(): return lax.all_gather(piece, 'seq', axis=0, tiled=True).astype(jnp.float32)  37.9 us
    dot_general x1, matrix products, local(): jnp.dot(normed_two_low, inner_weight, preferred_element_type=jnp.float32)  36 us
  transfers between devices with their start and end apart: 16, of which 8 were waited for; matrix products, arithmetic and copies ran while one was open for 15% of the time, Pallas kernels for 5%

profile of v1, /device:TPU:0, one launch (start us, length us, event | category | flops | bytes accessed | tf_op | source)
XLA Modules:
  0.0 929.9 jit_solution(6951204768414022191)
XLA Ops:
  7.3 3.0 constant_dynamic-slice_fusion.1
  11.5 3.0 collective-permute-start
  16.4 3.4 add_convert_fusion.6
  19.7 2.0 convolution_convert_fusion.8
  25.5 3.4 add_convert_fusion.8
  28.9 4.1 collective-permute-done
  33.5 2.0 add_convert_fusion.5
  35.5 2.0 convolution_convert_fusion.7
  38.8 2.3 copy.53
  41.1 2.5 add_convert_fusion.7
  43.7 3.8 pad_maximum_fusion.1.v_ref
  47.5 3.3 pad_maximum_fusion.k_ref
  50.8 47.7 %attend.1 = (bf16[1024,768]{1,0:T(8,128)(2,1)S(1)}, f32[6,2,1024]{2,1,0:T(2,128)S(1)}) custom-call(s32[5]{0:T(128)S(1)} %pad_add_fusion.info_ref, bf16[1024,768]{1,0:T(8,128)(2,1)S(1)} %pad_maximum_fusion.3.q_ref, bf16[2048,768]{1,0:T(8,128)(2,1)} %pad_maximum_fusion.k_ref, bf16[2048,768]{1,0:T(8,128)(2,1)} %pad_maximum_fusion.1.v_ref), custom_call_target="tpu_custom_call" | custom-call | flops 25769803776 | bytes 8388608 | tf_op jit(solution)/shard_map/attend/pallas_call | solution.py:75
  98.6 4.0 fusion.56
  103.4 36.0 %multiply_convert_fusion = (bf16[1024,3072]{1,0:T(8,128)(2,1)}, f32[1024,3072]{1,0:T(8,128)}, f32[1024,3072]{1,0:T(8,128)}) fusion(f32[3072]{0:T(1024)S(1)} %copy-done.46, bf16[768,3072]{1,0:T(8,128)(2,1)S(1)} %bitcast.67, f32[1024,768]{0,1:T(8,128)S(1)} %get-tuple-element.103, f32[768]{0:T(1024)S(1)} %copy-done.52, f32[768]{0:T(1024)S(1)} %copy-done.36, ...), kind=kOutput, calls=%fused_computation.4 | convolution fusion | flops 5043388416 | bytes 39348224 | tf_op jit(solution)/shard_map/dot_general | solution.py:273
  139.4 18.2 %convert_reduce_fusion = (f32[3072]{0:T(1024)}, bf16[1024,3072]{1,0:T(8,128)(2,1)}) fusion(f32[1024,3072]{1,0:T(8,128)} %get-tuple-element.101, bf16[3072,768]{1,0:T(8,128)(2,1)} %param.33, f32[1024]{0:T(1024)S(1)} %fusion.39, bf16[512,768]{0,1:T(8,128)(2,1)} %collective-permute-done.6, bf16[512,768]{0,1:T(8,128)(2,1)S(1)} %bitcast.58, ...), kind=kOutput, calls=%fused_computation.2 | convolution fusion | flops 4890031104 | bytes 37777408 | tf_op jit(solution)/shard_map/td,fd->tf/dot_general | solution.py:285
  157.6 10.3 %fusion.58 = (f32[768]{0:T(1024)}, f32[1024,768]{1,0:T(8,128)}) fusion(bf16[1024,3072]{1,0:T(8,128)(2,1)} %get-tuple-element.124, bf16[768,3072]{1,0:T(8,128)(2,1)} %param.31), kind=kOutput, calls=%fused_computation.128 | convolution fusion | flops 4832623616 | bytes 14158848 | tf_op jit(solution)/shard_map/tf,df->td/dot_general | solution.py:293
  167.9 3.5 copy.55
  171.5 13.9 %fusion.18 = (f32[]{:T(128)}, f32[]{:T(128)}, f32[1024]{0:T(1024)S(1)}, f32[768]{0:T(1024)}, f32[768]{0:T(1024)}, /*index=5*/f32[]{:T(128)}, bf16[1024,768]{0,1:T(8,128)(2,1)}) fusion(f32[768]{0:T(1024)S(1)} %copy-done.49, f32[1024]{0:T(1024)S(1)} %fusion.39, f32[1024,768]{0,1:T(8,128)} %copy-done.12, f32[1024,768]{0,1:T(8,128)} %copy.55, ...), kind=kOutput, calls=%fused_computation.39 | convolution fusion | flops 4853855232 | bytes 23624716 | tf_op jit(solution)/shard_map/dot_general | solution.py:276
  186.2 3.0 convert_reduce_fusion.3
  190.7 84.0 %attend_back.1 = (bf16[1024,768]{1,0:T(8,128)(2,1)S(1)}, bf16[2048,768]{1,0:T(8,128)(2,1)}, bf16[2048,768]{1,0:T(8,128)(2,1)}) custom-call(s32[5]{0:T(128)S(1)} %copy-done.7, bf16[1024,768]{1,0:T(8,128)(2,1)S(1)} %copy-done.3, bf16[2048,768]{1,0:T(8,128)(2,1)} %pad_maximum_fusion.k_ref, bf16[2048,768]{1,0:T(8,128)(2,1)} %pad_maximum_fusion.1.v_ref, ...), custom_call_target="tpu_custom_call" | custom-call | flops 64424509440 | bytes 16777216 | tf_op jit(solution)/shard_map/attend_back/pallas_call | solution.py:158
  274.7 2.8 slice.35
  279.3 2.5 convolution_convert_fusion.3
  282.1 2.8 fusion.59
  285.1 3.0 fusion.36
  288.2 5.2 fusion.52
  293.4 2.6 convolution_convert_fusion.6
  296.1 4.6 convolution_convert_fusion.5
  300.8 4.7 convolution_convert_fusion.4
  305.6 9.9 %convolution_convert_fusion.1 = bf16[768,3072]{1,0:T(8,128)(2,1)} fusion(bf16[1024,3072]{1,0:T(8,128)(2,1)} %get-tuple-element.124, f32[1024,768]{0,1:T(8,128)} %copy-done.12, f32[768]{0:T(1024)S(1)} %copy-done.53, f32[768]{0:T(1024)S(1)} %copy-done.37, f32[1024]{0:T(1024)S(1)} %fusion.40, f32[1024]{0:T(1024)S(1)} %broadcast_multiply_fusion.1), kind=kOutput, calls=%fused_computation.19 | convolution fusion | flops 4838129664 | bytes 14170112 | tf_op jit(solution)/shard_map/td,tf->df/dot_general | solution.py:289
  315.8 9.2 convolution_convert_fusion
  325.1 2.8 slice_bitcast_fusion.1
  331.5 2.9 add_convert_fusion.1
  337.4 13.3 %collective-permute-done.5 = bf16[512,768]{0,1:T(8,128)(2,1)} collective-permute-done((bf16[512,768]{0,1:T(8,128)(2,1)}, bf16[512,768]{0,1:T(8,128)(2,1)}, u32[]{:S(2)}, u32[]{:S(2)}) %collective-permute-start.5) | collective-permute-done | bytes 786464 | tf_op jit(solution)/shard_map/ppermute | solution.py:229
  354.0 28.2 %reduce-scatter.13.cloned.1.call-done = bf16[24,768]{1,0:T(8,128)(2,1)} async-done(((bf16[768,768]{1,0:T(8,128)(2,1)}), bf16[24,768]{1,0:T(8,128)(2,1)}) %reduce-scatter.13.cloned.1.call-update) | async-done | bytes 36880 | tf_op jit(solution)/shard_map/reduce_scatter | solution.py:361
  382.2 5.7 all_gather.21
  388.5 2.4 convert_reduce_fusion.4
  390.9 41.7 %all-reduce = (f32[768]{0:T(1024)}, f32[768]{0:T(1024)}, f32[768]{0:T(1024)}, f32[768]{0:T(1024)}, f32[768]{0:T(1024)}, /*index=5*/f32[768]{0:T(1024)}, f32[768]...) all-reduce(f32[768]{0:T(1024)S(1)} %get-tuple-element.72, ...), channel_id=1, replica_groups=mesh['dp'=8,'seq'=4] {'dp','seq'}, use_global_device_ids=true, to_apply=%region_13.14 | all-reduce | flops 9220 | bytes 73760 | tf_op jit(solution)/shard_map/psum | solution.py:336
  438.6 45.3 %reduce-scatter.7.cloned.1.call-done = bf16[24,768]{1,0:T(8,128)(2,1)} async-done(((bf16[768,768]{1,0:T(8,128)(2,1)}), bf16[24,768]{1,0:T(8,128)(2,1)}) %reduce-scatter.7.cloned.1.call-update) | async-done | bytes 36880 | tf_op jit(solution)/shard_map/reduce_scatter | solution.py:361
  483.9 5.7 all_gather.18
  490.3 95.4 %reduce-scatter.9.cloned.1.call-done = bf16[24,768]{1,0:T(8,128)(2,1)} async-done(((bf16[768,768]{1,0:T(8,128)(2,1)}), bf16[24,768]{1,0:T(8,128)(2,1)}) %reduce-scatter.9.cloned.1.call-update) | async-done | bytes 36880 | tf_op jit(solution)/shard_map/reduce_scatter | solution.py:361
  585.7 5.7 all_gather.19
  592.1 94.7 %reduce-scatter.11.cloned.1.call-done = bf16[24,768]{1,0:T(8,128)(2,1)} async-done(((bf16[768,768]{1,0:T(8,128)(2,1)}), bf16[24,768]{1,0:T(8,128)(2,1)}) %reduce-scatter.11.cloned.1.call-update) | async-done | bytes 36880 | tf_op jit(solution)/shard_map/reduce_scatter | solution.py:361
  686.8 5.7 all_gather.20
  693.2 105.5 %reduce-scatter.15.cloned.1.call-done = bf16[24,3072]{1,0:T(8,128)(2,1)} async-done(((bf16[768,3072]{1,0:T(8,128)(2,1)}), bf16[24,3072]{1,0:T(8,128)(2,1)}) %reduce-scatter.15.cloned.1.call-update) | async-done | bytes 147472 | tf_op jit(solution)/shard_map/reduce_scatter | solution.py:361
  798.7 7.6 all_gather.22
  807.4 103.0 %reduce-scatter.17.cloned.1.call-done = bf16[96,768]{1,0:T(8,128)(2,1)} async-done(((bf16[3072,768]{1,0:T(8,128)(2,1)}), bf16[96,768]{1,0:T(8,128)(2,1)}) %reduce-scatter.17.cloned.1.call-update) | async-done | bytes 147472 | tf_op jit(solution)/shard_map/reduce_scatter | solution.py:361
  910.4 7.7 all_gather.23
  (187 shorter events, 32.5 us)
Async XLA Ops:
  7.2 91.4 %copy-start = (bf16[768,768]{1,0:T(8,128)(2,1)S(1)}, bf16[768,768]{1,0:T(8,128)(2,1)}, u32[]{:S(2)}) copy-start(bf16[768,768]{1,0:T(8,128)(2,1)} %param.27) | copy-start | bytes 3538948
  7.2 374.9 %reduce-scatter.13.cloned.1.call-start = ((), (), s32[]{:S(2)}) async-start(), calls=%async_computation.9 | async-start | bytes 1216512 | tf_op jit(solution)/shard_map/reduce_scatter | solution.py:361
  10.3 6.1 copy-start.30
  10.3 6.1 copy-start.47
  10.3 6.1 copy-start.50
  11.5 21.6 %collective-permute-start = (bf16[512,768]{0,1:T(8,128)(2,1)}, bf16[512,768]{0,1:T(8,128)(2,1)S(1)}, u32[]{:S(2)}, u32[]{:S(2)}) collective-permute-start(bf16[512,768]{0,1:T(8,128)(2,1)} %bitcast.63), channel_id=1, source_target_pairs={{0,2},{1,3},{2,0},{3,1},{4,6},{5,7},{6,4},{7,5},{8,10},{9,11},{10,... | collective-permute-start | bytes 2359304 | tf_op jit(solution)/shard_map/ppermute | solution.py:223
  15.6 123.8 %collective-permute-start.6 = (bf16[512,768]{0,1:T(8,128)(2,1)}, bf16[512,768]{0,1:T(8,128)(2,1)}, u32[]{:S(2)}, u32[]{:S(2)}) collective-permute-start(bf16[512,768]{0,1:T(8,128)(2,1)} %bitcast.62), channel_id=1, source_target_pairs={{0,2},{1,3},{2,0},{3,1},{4,6},{5,7},{6,4},{7,5},{8,10},{9,11},{10,... | collective-permute-start | bytes 2359304 | tf_op jit(solution)/shard_map/ppermute | solution.py:223
  15.9 82.7 %copy-start.8 = (bf16[1,512,768]{1,2,0:T(8,128)(2,1)}, bf16[1,512,768]{1,2,0:T(8,128)(2,1)S(1)}, u32[]{:S(2)}) copy-start(bf16[1,512,768]{1,2,0:T(8,128)(2,1)S(1)} %copy.50) | copy-start | bytes 2359300
  19.7 5.8 copy-start.48
  19.7 24.0 %collective-permute-start.3 = (bf16[512,768]{1,0:T(8,128)(2,1)}, bf16[512,768]{1,0:T(8,128)(2,1)}, u32[]{:S(2)}, u32[]{:S(2)}) collective-permute-start(bf16[512,768]{1,0:T(8,128)(2,1)} %add_convert_fusion.6), channel_id=1, source_target_pairs={{0,1},{1,0},{2,3},{3,2},{4,5},{5,4},{6,7},{7,6},{8,9},{9,8},{10,11... | collective-permute-start | bytes 2359304 | tf_op jit(solution)/shard_map/ppermute | solution.py:260
  21.8 25.7 %collective-permute-start.1 = (bf16[512,768]{1,0:T(8,128)(2,1)}, bf16[512,768]{1,0:T(8,128)(2,1)}, u32[]{:S(2)}, u32[]{:S(2)}) collective-permute-start(bf16[512,768]{1,0:T(8,128)(2,1)} %convolution_convert_fusion.8), channel_id=1, source_target_pairs={{0,1},{1,0},{2,3},{3,2},{4,5},{5,4},{6,7},{7,6},{8,9},{9,8},{10,11... | collective-permute-start | bytes 2359304 | tf_op jit(solution)/shard_map/ppermute | solution.py:260
  24.8 8.4 copy-start.26
  24.8 8.4 copy-start.28
  25.5 8.0 copy-start.44
  33.1 8.0 copy-start.14
  35.5 8.2 collective-permute-start.4
  37.6 10.0 %collective-permute-start.2 = (bf16[512,768]{1,0:T(8,128)(2,1)}, bf16[512,768]{1,0:T(8,128)(2,1)}, u32[]{:S(2)}, u32[]{:S(2)}) collective-permute-start(bf16[512,768]{1,0:T(8,128)(2,1)} %convolution_convert_fusion.7), channel_id=1, source_target_pairs={{0,1},{1,0},{2,3},{3,2},{4,5},{5,4},{6,7},{7,6},{8,9},{9,8},{10,11... | collective-permute-start | bytes 2359304 | tf_op jit(solution)/shard_map/ppermute | solution.py:260
  38.8 12.0 %copy-start.6 = (s32[5]{0:T(128)}, s32[5]{0:T(128)S(1)}, u32[]{:S(2)}) copy-start(s32[5]{0:T(128)S(1)} %pad_add_fusion.info_ref) | copy-start | bytes 64
  43.7 7.1 copy-start.2
  50.8 47.8 %copy-start.15 = (bf16[512,768]{0,1:T(8,128)(2,1)S(1)}, bf16[512,768]{0,1:T(8,128)(2,1)}, u32[]{:S(2)}) copy-start(bf16[512,768]{0,1:T(8,128)(2,1)} %copy-done.14) | copy-start | bytes 2359300
  50.8 47.8 %copy-start.35 = (f32[768]{0:T(1024)S(1)}, f32[768]{0:T(1024)}, u32[]{:S(2)}) copy-start(f32[768]{0:T(1024)} %param.28) | copy-start | bytes 9220
  98.6 4.5 slice-start
  98.6 4.4 slice-start.1
  102.6 36.8 %copy-start.12 = (f32[1024,768]{0,1:T(8,128)}, f32[1024,768]{0,1:T(8,128)S(1)}, u32[]{:S(2)}) copy-start(f32[1024,768]{0,1:T(8,128)S(1)} %get-tuple-element.103) | copy-start | bytes 9437188
  103.4 36.0 %copy-start.19 = (bf16[1,512,768]{1,2,0:T(8,128)(2,1)S(1)}, bf16[1,512,768]{1,2,0:T(8,128)(2,1)}, u32[]{:S(2)}) copy-start(bf16[1,512,768]{1,2,0:T(8,128)(2,1)} %copy.53) | copy-start | bytes 2359300
  171.5 13.9 %copy-start.13 = (f32[1024,768]{0,1:T(8,128)S(1)}, f32[1024,768]{0,1:T(8,128)}, u32[]{:S(2)}) copy-start(f32[1024,768]{0,1:T(8,128)} %copy-done.12) | copy-start | bytes 9437188
  171.5 13.9 %copy-start.18 = (f32[1024,768]{0,1:T(8,128)S(1)}, f32[1024,768]{0,1:T(8,128)}, u32[]{:S(2)}) copy-start(f32[1024,768]{0,1:T(8,128)} %copy.55) | copy-start | bytes 9437188
  274.7 4.6 copy-start.5
  277.5 7.5 collective-permute-start.7
  278.8 9.3 %collective-permute-start.8 = (bf16[1024,768]{1,0:T(8,128)(2,1)}, bf16[1024,768]{1,0:T(8,128)(2,1)}, u32[]{:S(2)}, u32[]{:S(2)}) collective-permute-start(bf16[1024,768]{1,0:T(8,128)(2,1)} %slice.37), channel_id=1, source_target_pairs={{0,1},{1,0},{2,3},{3,2},{4,5},{5,4},{6,7},{7,6},{8,9},{9,8},{10,11... | collective-permute-start | bytes 4718600 | tf_op jit(solution)/shard_map/ppermute | solution.py:311
  281.8 202.1 %reduce-scatter.7.cloned.1.call-start = ((), (), s32[]{:S(2)}) async-start(), calls=%async_computation.6 | async-start | bytes 1216512 | tf_op jit(solution)/shard_map/reduce_scatter | solution.py:361
  288.1 5.3 copy-start.51
  296.0 289.7 %reduce-scatter.9.cloned.1.call-start = ((), (), s32[]{:S(2)}) async-start(), calls=%async_computation.7 | async-start | bytes 1216512 | tf_op jit(solution)/shard_map/reduce_scatter | solution.py:361
  300.8 4.8 copy-start.37
  300.8 4.8 copy-start.53
  300.8 386.1 %reduce-scatter.11.cloned.1.call-start = ((), (), s32[]{:S(2)}) async-start(), calls=%async_computation.8 | async-start | bytes 1216512 | tf_op jit(solution)/shard_map/reduce_scatter | solution.py:361
  305.5 493.2 %reduce-scatter.15.cloned.1.call-start = ((), (), s32[]{:S(2)}) async-start(), calls=%async_computation.10 | async-start | bytes 4866048 | tf_op jit(solution)/shard_map/reduce_scatter | solution.py:361
  315.5 594.9 %reduce-scatter.17.cloned.1.call-start = ((), (), s32[]{:S(2)}) async-start(), calls=%async_computation.11 | async-start | bytes 4866048 | tf_op jit(solution)/shard_map/reduce_scatter | solution.py:361
  325.1 4.8 copy-start.17
  327.8 22.8 %collective-permute-start.5 = (bf16[512,768]{0,1:T(8,128)(2,1)}, bf16[512,768]{0,1:T(8,128)(2,1)}, u32[]{:S(2)}, u32[]{:S(2)}) collective-permute-start(bf16[512,768]{0,1:T(8,128)(2,1)} %get-tuple-element.111), channel_id=1, source_target_pairs={{0,2},{1,3},{2,0},{3,1},{4,6},{5,7},{6,4},{7,5},{8,10},{9,11},{10,... | collective-permute-start | bytes 2359304 | tf_op jit(solution)/shard_map/ppermute | solution.py:229
  334.5 16.2 %copy-start.23 = (bf16[1,512,768]{1,2,0:T(8,128)(2,1)S(1)}, bf16[1,512,768]{1,2,0:T(8,128)(2,1)}, u32[]{:S(2)}) copy-start(bf16[1,512,768]{1,2,0:T(8,128)(2,1)} %get-tuple-element.110) | copy-start | bytes 2359300
  335.5 99.9 %collective-permute-start.9 = (bf16[512,768]{0,1:T(8,128)(2,1)}, bf16[512,768]{0,1:T(8,128)(2,1)}, u32[]{:S(2)}, u32[]{:S(2)}) collective-permute-start(bf16[512,768]{0,1:T(8,128)(2,1)} %get-tuple-element.106), channel_id=1, source_target_pairs={{0,2},{1,3},{2,0},{3,1},{4,6},{5,7},{6,4},{7,5},{8,10},{9,11},{10,... | collective-permute-start | bytes 2359304 | tf_op jit(solution)/shard_map/ppermute | solution.py:229
  352.3 38.6 %copy-start.33 = (f32[768]{0:T(1024)S(1)}, f32[768]{0:T(1024)}, u32[]{:S(2)}) copy-start(f32[768]{0:T(1024)} %get-tuple-element.96) | copy-start | bytes 9220
  352.3 38.6 %copy-start.34 = (f32[3072]{0:T(1024)S(1)}, f32[3072]{0:T(1024)}, u32[]{:S(2)}) copy-start(f32[3072]{0:T(1024)} %get-tuple-element.123) | copy-start | bytes 36868
  352.4 38.6 %copy-start.38 = (f32[768]{0:T(1024)S(1)}, f32[768]{0:T(1024)}, u32[]{:S(2)}) copy-start(f32[768]{0:T(1024)} %get-tuple-element.121) | copy-start | bytes 9220
  352.4 38.6 %copy-start.39 = (f32[768]{0:T(1024)S(1)}, f32[768]{0:T(1024)}, u32[]{:S(2)}) copy-start(f32[768]{0:T(1024)} %get-tuple-element.77) | copy-start | bytes 9220
  352.4 38.6 %copy-start.40 = (f32[768]{0:T(1024)S(1)}, f32[768]{0:T(1024)}, u32[]{:S(2)}) copy-start(f32[768]{0:T(1024)} %get-tuple-element.81) | copy-start | bytes 9220
  489.6 429.6 %copy-start.1 = (bf16[768,768]{1,0:T(8,128)(2,1)S(1)}, bf16[768,768]{1,0:T(8,128)(2,1)}, u32[]{:S(2)}) copy-start(bf16[768,768]{1,0:T(8,128)(2,1)} %param.27) | copy-start | bytes 3538948
  (25 other events, 64.0 us)
Sparse Core Ops, SparseCore 0:
  281.9 100.1 reduce-scatter.12
  387.8 96.0 reduce-scatter.6
  489.6 96.0 reduce-scatter.8
  590.7 96.1 reduce-scatter.10
  692.2 106.4 reduce-scatter.14
  804.0 106.3 reduce-scatter.16

commit v2 on v1

--- a/solution.py
+++ b/solution.py
@@ -182,6 +182,205 @@
         ),
         name="attend_back",
     )(info, queries, keys, values, grad_out, out, log_sums)
+
+
+MESH_IDS = pl.DeviceIdType.MESH
+AXES = ("zhi", "zlo", "x", "y")
+COLORS = (("y", "x", "zlo", "zhi"), ("x", "y", "zlo", "zhi"), ("zlo", "zhi", "y", "x"))
+
+
+def where_am_i():
+    data = lax.axis_index("dp")
+    seq = lax.axis_index("seq")
+    bits = {
+        "zhi": data // 4,
+        "zlo": (data // 2) % 2,
+        "x": data % 2,
+        "y": seq // 2,
+        "core": seq % 2,
+    }
+
+    def across(axis):
+        if axis == "core":
+            return (data, seq + 1 - 2 * bits["core"])
+        if axis == "y":
+            return (data, seq + 2 - 4 * bits["y"])
+        step = {"zhi": 4, "zlo": 2, "x": 1}[axis]
+        return (data + step - 2 * step * bits[axis], seq)
+
+    return bits, across
+
+
+def spot_of(piece, order):
+    bits = {axis: (piece >> (3 - k)) & 1 for k, axis in enumerate(AXES)}
+    return sum(bits[axis] << (3 - k) for k, axis in enumerate(order))
+
+
+class Color:
+    def __init__(self, source, acc, lands, gathers, sems, order):
+        self.source, self.acc, self.lands, self.gathers = source, acc, lands, gathers
+        self.sems, self.order = sems, order
+        self.pieces, self.rows, self.cols = acc.shape
+        self.bits, self.across = where_am_i()
+        self.base = 0
+
+    def remote(self, src, dst, slot, axis):
+        return pltpu.make_async_remote_copy(
+            src_ref=src,
+            dst_ref=dst,
+            send_sem=self.sems.at[0, slot],
+            recv_sem=self.sems.at[1, slot],
+            device_id=self.across(axis),
+            device_id_type=MESH_IDS,
+        )
+
+    def begin(self):
+        core = self.bits["core"]
+        mine = pl.ds(pl.multiple_of(core * self.cols, 128), self.cols)
+        theirs = pl.ds(pl.multiple_of((1 - core) * self.cols, 128), self.cols)
+        for piece in range(self.pieces):
+            spot = spot_of(piece, self.order)
+            span = pl.ds(piece * self.rows, self.rows)
+            self.remote(
+                self.source.at[span, theirs], self.lands[0].at[spot], 0, "core"
+            ).start()
+            pltpu.make_async_copy(
+                self.source.at[span, mine], self.acc.at[spot], self.sems.at[0, 7]
+            ).start()
+
+    def add(self, count, land):
+        base = self.base
+
+        @pl.loop(0, count)
+        def _(index):
+            total = self.acc[base + index].astype(jnp.float32) + land[index].astype(jnp.float32)
+            self.acc[base + index] = total.astype(jnp.bfloat16)
+
+    def send(self, stage):
+        axis = self.order[stage]
+        half = self.pieces >> (stage + 1)
+        me = self.bits[axis]
+        self.copy = self.remote(
+            self.acc.at[pl.ds(self.base + (1 - me) * half, half)],
+            self.lands[stage + 1],
+            stage + 1,
+            axis,
+        )
+        self.copy.start()
+        self.base = self.base + me * half
+
+    def step(self, stage):
+        if stage == 0:
+            whole = self.remote(self.lands[0], self.lands[0], 0, "core")
+            pltpu.make_async_copy(self.acc, self.acc, self.sems.at[0, 7]).wait()
+            whole.wait_send()
+            whole.wait_recv()
+            self.add(self.pieces, self.lands[0])
+            self.send(0)
+        elif stage <= 4:
+            self.copy.wait()
+            self.add(self.pieces >> stage, self.lands[stage])
+            if stage < 4:
+                self.send(stage)
+            else:
+                y = self.bits["y"]
+                self.gathers[0][y] = self.acc[self.base]
+                self.copy = self.remote(self.acc.at[self.base], self.gathers[0].at[y], 5, "y")
+                self.copy.start()
+        elif stage == 5:
+            self.copy.wait()
+            self.copy = self.remote(self.gathers[0], self.gathers[1], 6, "core")
+            self.copy.start()
+        else:
+            self.copy.wait()
+
+
+def vector_sum(source, held, lands, sems, bits_across):
+    bits, across = bits_across
+    held[...] = source[...]
+    for slot, axis in enumerate(("core", "y", "x", "zlo", "zhi")):
+        copy = pltpu.make_async_remote_copy(
+            src_ref=held,
+            dst_ref=lands.at[slot],
+            send_sem=sems.at[0, slot],
+            recv_sem=sems.at[1, slot],
+            device_id=across(axis),
+            device_id_type=MESH_IDS,
+        )
+        copy.start()
+        yield
+        copy.wait()
+        held[...] = held[...] + lands[slot]
+
+
+def reduce_body(count, orders, *refs):
+    sources, vector = refs[:count], refs[count]
+    outs = refs[count + 1 : count + 1 + 2 * count]
+    vector_out = refs[3 * count + 1]
+    scratch = refs[3 * count + 2 :]
+    bits, across = where_am_i()
+    barrier = pltpu.get_barrier_semaphore()
+    for axis in ("core", *AXES):
+        pl.semaphore_signal(barrier, inc=1, device_id=across(axis), device_id_type=MESH_IDS)
+    pl.semaphore_wait(barrier, 5)
+    colors = []
+    for index in range(count):
+        acc, *lands = scratch[7 * index : 7 * index + 6]
+        colors.append(
+            Color(
+                sources[index],
+                acc,
+                lands,
+                outs[2 * index : 2 * index + 2],
+                scratch[7 * index + 6],
+                orders[index],
+            )
+        )
+    vector_lands, vector_sems = scratch[7 * count :]
+    small = vector_sum(vector, vector_out, vector_lands, vector_sems, (bits, across))
+    for color in colors:
+        color.begin()
+    next(small)
+    for stage in range(7):
+        for color in colors:
+            color.step(stage)
+        next(small, None)
+
+
+def reduce_all(arrays, orders, vector, collective):
+    scratch = []
+    outs = []
+    for array in arrays:
+        rows, cols = array.shape[0] // 16, array.shape[1] // 2
+        scratch.append(pltpu.VMEM((16, rows, cols), jnp.bfloat16))
+        for size in (16, 8, 4, 2, 1):
+            scratch.append(pltpu.VMEM((size, rows, cols), jnp.bfloat16))
+        scratch.append(pltpu.SemaphoreType.DMA((2, 8)))
+        outs += [jax.ShapeDtypeStruct((2, rows, cols), jnp.bfloat16)] * 2
+    scratch.append(pltpu.VMEM((5, *vector.shape), jnp.float32))
+    scratch.append(pltpu.SemaphoreType.DMA((2, 5)))
+    outs.append(jax.ShapeDtypeStruct(vector.shape, jnp.float32))
+    vmem = pl.BlockSpec(memory_space=pltpu.VMEM)
+    got = pl.pallas_call(
+        functools.partial(reduce_body, len(arrays), orders),
+        out_shape=outs,
+        in_specs=[pl.BlockSpec(memory_space=pl.ANY)] * len(arrays) + [vmem],
+        out_specs=[vmem] * len(outs),
+        scratch_shapes=scratch,
+        compiler_params=pltpu.CompilerParams(
+            collective_id=collective, has_side_effects=True, vmem_limit_bytes=60 << 20
+        ),
+        name="reduce_all",
+    )(*arrays, vector)
+    core = lax.axis_index("seq") % 2
+    sums = []
+    for index, array in enumerate(arrays):
+        mine, other = got[2 * index], got[2 * index + 1]
+        rows = array.shape[0] // 8
+        left = jnp.where(core == 0, mine, other).reshape(rows, -1)
+        right = jnp.where(core == 0, other, mine).reshape(rows, -1)
+        sums.append(jnp.concatenate([left, right], axis=1).astype(jnp.float32))
+    return sums, got[-1]
 
 
 def local(
@@ -315,14 +514,12 @@
 
     grad_k_tok = join(grad_k_part)
     grad_v_tok = join(grad_v_part)
-    grad_query_weight = jnp.einsum(
-        "td,te->de", normed_one_low, grad_q_tok, preferred_element_type=jnp.float32
-    )
-    grad_key_weight = jnp.einsum(
-        "td,te->de", normed_one_low, grad_k_tok, preferred_element_type=jnp.float32
-    )
-    grad_value_weight = jnp.einsum(
-        "td,te->de", normed_one_low, grad_v_tok, preferred_element_type=jnp.float32
+    grad_qkv = jnp.concatenate(
+        [
+            dot(normed_one_low, grad, TN).astype(jnp.bfloat16)
+            for grad in (grad_q_tok, grad_k_tok, grad_v_tok)
+        ],
+        axis=1,
     )
     grad_query_bias = jnp.sum(grad_q_tok, axis=0, dtype=jnp.float32)
     grad_value_bias = jnp.sum(grad_v_tok, axis=0, dtype=jnp.float32)
@@ -333,42 +530,66 @@
     )
     grad_in_norm, grad_first_gain, grad_first_shift = norm_one_back(grad_normed_one)
     grad_inputs = give_back((grad_hidden + grad_in_norm).astype(jnp.bfloat16))
-    totals = lax.psum(
-        (
-            jnp.sum(stream * stream),
-            jnp.sum(keep_rows * branch_attn * branch_attn),
-            jnp.sum(keep_rows * branch_ffn * branch_ffn),
-            jnp.sum(keep_rows),
-            grad_first_gain,
-            grad_first_shift,
-            grad_query_bias,
-            grad_value_bias,
-            grad_output_bias,
-            grad_second_gain,
-            grad_second_shift,
-            grad_inner_bias,
-            grad_outer_bias,
-        ),
-        ("dp", "seq"),
-    )
+    vectors = (
+        jnp.stack(
+            [
+                jnp.sum(stream * stream),
+                jnp.sum(keep_rows * branch_attn * branch_attn),
+                jnp.sum(keep_rows * branch_ffn * branch_ffn),
+                jnp.sum(keep_rows),
+            ]
+        ),
+        grad_first_gain,
+        grad_first_shift,
+        grad_query_bias,
+        grad_value_bias,
+        grad_output_bias,
+        grad_second_gain,
+        grad_second_shift,
+        grad_inner_bias,
+        grad_outer_bias,
+    )
+    data_groups = lax.axis_size("dp")
+    packed = jnp.concatenate([jnp.pad(vectors[0], (0, 124)), *vectors[1:]])
+    size = packed.shape[0]
+    packed = jnp.pad(packed, (0, -size % 1024)).reshape(-1, 128)
+    low = jnp.bfloat16
+    if data_groups == 8 and groups == 4:
+        (summed_outer, summed_inner, qkv, summed_output), packed = reduce_all(
+            (
+                grad_outer_weight.astype(low),
+                grad_inner_weight.astype(low),
+                grad_qkv.astype(low),
+                grad_output_weight.astype(low),
+            ),
+            (COLORS[0], COLORS[1], COLORS[2], COLORS[2]),
+            packed,
+            1,
+        )
+    else:
+
+        def reduced(partial):
+            piece = lax.psum_scatter(
+                partial.astype(low), ("dp", "seq"), scatter_dimension=0, tiled=True
+            )
+            return lax.all_gather(piece, "seq", axis=0, tiled=True).astype(jnp.float32)
+
+        summed_outer = reduced(grad_outer_weight)
+        summed_inner = reduced(grad_inner_weight)
+        summed_output = reduced(grad_output_weight)
+        qkv = reduced(grad_qkv)
+        packed = lax.psum(packed, ("dp", "seq"))
+    summed_query, summed_key, summed_value = jnp.split(qkv, 3, axis=1)
+    packed = packed.reshape(-1)
+    totals = [packed[0], packed[1], packed[2], packed[3]]
+    at = 128
+    for item in vectors[1:]:
+        totals.append(packed[at : at + item.shape[0]])
+        at += item.shape[0]
     denominator = totals[3] * width
     stream_scale = jnp.sqrt(totals[0] / denominator)
     attention_scale = jnp.sqrt(totals[1] / denominator)
     feedforward_scale = jnp.sqrt(totals[2] / denominator)
-    data_groups = lax.axis_size("dp")
-
-    def reduced(partial):
-        piece = lax.psum_scatter(
-            partial.astype(jnp.bfloat16), ("dp", "seq"), scatter_dimension=0, tiled=True
-        )
-        return lax.all_gather(piece, "seq", axis=0, tiled=True).astype(jnp.float32)
-
-    summed_query = reduced(grad_query_weight)
-    summed_key = reduced(grad_key_weight)
-    summed_value = reduced(grad_value_weight)
-    summed_output = reduced(grad_output_weight)
-    summed_inner = reduced(grad_inner_weight)
-    summed_outer = reduced(grad_outer_weight)
     return (
         result,
         grad_inputs,

time: 937 us -> 476 us (0.51)
  waiting for transfers between devices: 490 us -> 18.9 us
  Pallas kernels: 132 us -> 233 us
  blocking collectives: 79.6 us -> 0 us
  between operations: 21.5 us -> 8.12 us
    reduce_scatter x6 -> x0, waiting for transfers between devices: 472 us -> none  [reduced(): lax.psum_scatter(partial.astype(jnp.bfloat16), ('dp', 'seq'), scatter_dim...]
    pallas_call x0 -> x1, Pallas kernels: none -> 101 us  [reduce_all(): pl.pallas_call(functools.partial(reduce_body, len(arrays), orders), out_s...]
    psum x1 -> x0, blocking collectives: 41.7 us -> none  [local(): lax.psum((jnp.sum(stream * stream), jnp.sum(keep_rows * branch_attn * bra...]
    all_gather x6 -> x0, blocking collectives: 37.9 us -> none  [reduced(): return lax.all_gather(piece, 'seq', axis=0, tiled=True).astype(jnp.float32)]
  transfers between devices with their start and end apart: 16 -> 10, of which waited for: 8 -> 2; matrix products, arithmetic and copies ran while one was open for 15% -> 24% of each run, Pallas kernels for 5% -> 10%
where the time goes in v2:
time: 476 us; the launch traced here: 468 us
  Pallas kernels  233 us (49%)
  matrix products  136 us (29%)
  other arithmetic  34.7 us (7%)
  local copies, waits for them, and re-layouts  31.4 us (7%)
  waiting for transfers between devices  18.9 us (4%)
  between operations  8.12 us (2%)
  starting transfers between devices  6.43 us (1%)
    pallas_call x1, Pallas kernels, reduce_all(): pl.pallas_call(functools.partial(reduce_body, len(arrays), orders), out_s...  101 us
    pallas_call x1, Pallas kernels, attend_back(): pl.pallas_call(attend_back_body, grid_spec=pltpu.PrefetchScalarGridSpec(n...  84.1 us
    pallas_call x1, Pallas kernels, attend(): pl.pallas_call(attend_body, grid_spec=pltpu.PrefetchScalarGridSpec(num_sc...  47.7 us
    dot_general x1, matrix products, local(): jnp.dot(normed_two_low, inner_weight, preferred_element_type=jnp.float32)  36 us
    dot_general x1, matrix products, local(): jnp.einsum('td,fd->tf', grad_ffn_low, outer_weight, preferred_element_typ...  18.2 us
    ppermute x2, waiting for transfers between devices, give_back(): other = lax.ppermute(array[local_len:], 'seq', across)  15.9 us
    dot_general x1, matrix products, local(): jnp.dot(activated, outer_weight, preferred_element_type=jnp.float32)  14 us
    dot_general x1, matrix products, local(): jnp.einsum('tf,df->td', grad_inner_low, inner_weight, preferred_element_t...  9.77 us
  transfers between devices with their start and end apart: 10, of which 2 were waited for; matrix products, arithmetic and copies ran while one was open for 24% of the time, Pallas kernels for 10%

profile of v2, /device:TPU:0, one launch (start us, length us, event | category | flops | bytes accessed | tf_op | source)
XLA Modules:
  0.0 468.5 jit_solution(2633143964550150573)
XLA Ops:
  0.7 3.3 constant_dynamic-slice_fusion.1
  5.1 3.0 collective-permute-start
  8.1 1.4 copy.53
  10.0 3.4 add_convert_fusion.6
  13.5 2.0 convolution_convert_fusion.8
  18.4 1.3 iota_add_fusion
  20.4 3.4 add_convert_fusion.8
  23.8 2.9 collective-permute-done
  27.2 2.0 add_convert_fusion.5
  29.2 2.0 convolution_convert_fusion.7
  32.5 2.3 copy.56
  36.0 2.4 add_convert_fusion.7
  39.7 3.8 pad_maximum_fusion.2.v_ref
  43.5 3.3 pad_maximum_fusion.1.k_ref
  46.8 47.7 %attend.1 = (bf16[1024,768]{1,0:T(8,128)(2,1)S(1)}, f32[6,2,1024]{2,1,0:T(2,128)S(1)}) custom-call(s32[5]{0:T(128)S(1)} %pad_add_fusion.info_ref, bf16[1024,768]{1,0:T(8,128)(2,1)S(1)} %pad_maximum_fusion.4.q_ref, bf16[2048,768]{1,0:T(8,128)(2,1)} %pad_maximum_fusion.1.k_ref, bf16[2048,768]{1,0:T(8,128)(2,1)} %pad_maximum_fusion.2.v_ref), custom_call_target="tpu_custom_call" | custom-call | flops 25769803776 | bytes 8388608 | tf_op jit(solution)/shard_map/attend/pallas_call | solution.py:75
  94.6 4.1 fusion.56
  99.5 36.0 %multiply_convert_fusion = (bf16[1024,3072]{1,0:T(8,128)(2,1)}, f32[1024,3072]{1,0:T(8,128)}, f32[1024,3072]{1,0:T(8,128)}) fusion(f32[3072]{0:T(1024)S(1)} %copy-done.46, bf16[768,3072]{1,0:T(8,128)(2,1)S(1)} %bitcast.114, f32[1024,768]{0,1:T(8,128)S(1)} %get-tuple-element.108, f32[768]{0:T(1024)S(1)} %copy-done.50, f32[768]{0:T(1024)S(1)} %copy-done.38, ...), kind=kOutput, calls=%fused_computation.4 | convolution fusion | flops 5043388416 | bytes 39348224 | tf_op jit(solution)/shard_map/dot_general | solution.py:472
  135.5 18.2 %convert_reduce_fusion = (f32[3072]{0:T(1024)}, bf16[1024,3072]{1,0:T(8,128)(2,1)}) fusion(f32[1024,3072]{1,0:T(8,128)} %get-tuple-element.106, bf16[3072,768]{1,0:T(8,128)(2,1)} %param.33, f32[1024]{0:T(1024)S(1)} %fusion.39, bf16[512,768]{0,1:T(8,128)(2,1)} %collective-permute-done.6, bf16[512,768]{0,1:T(8,128)(2,1)S(1)} %bitcast.94, ...), kind=kOutput, calls=%fused_computation.2 | convolution fusion | flops 4890031104 | bytes 37777408 | tf_op jit(solution)/shard_map/td,fd->tf/dot_general | solution.py:484
  153.6 9.8 %fusion.60 = (f32[768]{0:T(1024)S(1)}, f32[1024,768]{1,0:T(8,128)}) fusion(bf16[1024,3072]{1,0:T(8,128)(2,1)} %get-tuple-element.152, bf16[768,3072]{1,0:T(8,128)(2,1)} %param.31), kind=kOutput, calls=%fused_computation.167 | convolution fusion | flops 4832623616 | bytes 14158848 | tf_op jit(solution)/shard_map/tf,df->td/dot_general | solution.py:492
  163.4 3.5 copy.58
  167.0 14.0 %multiply_reduce_fusion = (f32[768]{0:T(1024)}, f32[1024]{0:T(1024)S(1)}, f32[]{:T(128)}, f32[]{:T(128)}, f32[768]{0:T(1024)}, /*index=5*/f32[]{:T(128)}, bf16[1024,768]{0,1:T(8,128)(2,1)}) fusion(f32[1024,768]{0,1:T(8,128)} %copy.58, f32[1024,768]{0,1:T(8,128)} %copy-done.12, f32[1024]{0:T(1024)S(1)} %fusion.40, f32[1024]{0:T(1024)S(1)} %broadcast_multiply_fusion.1, ...), kind=kOutput, calls=%fused_computation.44 | convolution fusion | flops 4853855232 | bytes 23624716 | tf_op jit(solution)/shard_map/dot_general | solution.py:475
  182.1 2.4 convert_reduce_fusion.3
  184.5 1.4 convolution_convert_fusion.2.do_ref
  186.0 84.1 %attend_back.1 = (bf16[1024,768]{1,0:T(8,128)(2,1)S(1)}, bf16[2048,768]{1,0:T(8,128)(2,1)}, bf16[2048,768]{1,0:T(8,128)(2,1)}) custom-call(s32[5]{0:T(128)S(1)} %copy-done.7, bf16[1024,768]{1,0:T(8,128)(2,1)S(1)} %copy-done.3, bf16[2048,768]{1,0:T(8,128)(2,1)} %pad_maximum_fusion.1.k_ref, bf16[2048,768]{1,0:T(8,128)(2,1)} %pad_maximum_fusion.2.v_ref, ...), custom_call_target="tpu_custom_call" | custom-call | flops 64424509440 | bytes 16777216 | tf_op jit(solution)/shard_map/attend_back/pallas_call | solution.py:158
  270.1 2.8 slice.101
  273.0 2.1 collective-permute-start.5
  275.1 8.9 %convolution_convert_fusion.1.refs_0_ = bf16[3072,768]{1,0:T(8,128)(2,1)} fusion(bf16[1024,3072]{1,0:T(8,128)(2,1)} %get-tuple-element.105, f32[1024]{0:T(1024)S(1)} %fusion.39, bf16[512,768]{0,1:T(8,128)(2,1)} %collective-permute-done.6, bf16[512,768]{0,1:T(8,128)(2,1)S(1)} %bitcast.96), kind=kOutput, calls=%fused_computation.19 | convolution fusion | flops 4838916096 | bytes 12587008 | tf_op jit(solution)/shard_map/tf,td->fd/dot_general | solution.py:480
  284.0 7.3 %convolution_convert_fusion.refs_1_ = bf16[768,3072]{1,0:T(8,128)(2,1)} fusion(bf16[1024,3072]{1,0:T(8,128)(2,1)S(1)} %bitcast.116, f32[1024,768]{0,1:T(8,128)S(1)} %copy-done.13, f32[768]{0:T(1024)S(1)} %copy-done.50, f32[768]{0:T(1024)S(1)} %copy-done.38, f32[1024]{0:T(1024)S(1)} %fusion.40, f32[1024]{0:T(1024)S(1)} %broadcast_multiply_fusion.1), kind=kOutput, calls=%fused_computation.18 | convolution fusion | flops 4838129664 | bytes 14170112 | tf_op jit(solution)/shard_map/td,tf->df/dot_general | solution.py:488
  293.2 2.7 constant_dynamic-update-slice_fusion.9
  295.9 3.1 fusion.61
  299.0 2.5 convolution_convert_fusion.3.refs_3_
  301.5 1.4 maximum_select_fusion
  302.9 2.6 copy.66
  305.5 3.8 fusion.36
  310.4 3.6 fusion.52
  314.1 1.9 fusion.14
  316.1 1.9 convert_reduce_fusion.4
  318.7 1.6 convolution_convert_fusion.6
  320.6 3.2 convolution_convert_fusion.5
  323.8 3.2 convolution_convert_fusion.4
  327.0 2.0 pad_maximum_fusion.refs_2_
  329.0 101.3 %reduce_all.1 = (bf16[2,192,384]{2,1,0:T(8,128)(2,1)}, bf16[2,192,384]{2,1,0:T(8,128)(2,1)}, bf16[2,48,1536]{2,1,0:T(8,128)(2,1)}, bf16[2,48,1536]{2,1,0:T(8,128...) custom-call(bf16[3072,768]{1,0:T(8,128)(2,1)} %convolution_convert_f, ...), custom_call_target="tpu_custom_call" | custom-call | tf_op jit(solution)/shard_map/reduce_all/pallas_call | solution.py:364
  430.3 1.6 slice_bitcast_fusion.3
  431.9 1.3 slice_bitcast_fusion.2
  433.2 1.4 fusion.58
  439.4 3.3 add_convert_fusion.1
  446.9 15.9 %collective-permute-done.9 = bf16[512,768]{0,1:T(8,128)(2,1)S(1)} collective-permute-done((bf16[512,768]{0,1:T(8,128)(2,1)S(1)}, bf16[512,768]{0,1:T(8,128)(2,1)S(1)}, u32[]{:S(2)}, u32[]{:S(2)}) %collective-permute-start.9) | collective-permute-done | bytes 786464 | tf_op jit(solution)/shard_map/ppermute | solution.py:428
  463.1 1.6 copy.67
  (189 shorter events, 21.9 us)
Async XLA Ops:
  0.7 93.9 %copy-start = (bf16[768,768]{1,0:T(8,128)(2,1)S(1)}, bf16[768,768]{1,0:T(8,128)(2,1)}, u32[]{:S(2)}) copy-start(bf16[768,768]{1,0:T(8,128)(2,1)} %param.27) | copy-start | bytes 3538948
  4.0 6.0 %copy-start.33 = (f32[768]{0:T(1024)S(1)}, f32[768]{0:T(1024)}, u32[]{:S(2)}) copy-start(f32[768]{0:T(1024)} %param.20) | copy-start | bytes 9220
  5.1 21.6 %collective-permute-start = (bf16[512,768]{0,1:T(8,128)(2,1)}, bf16[512,768]{0,1:T(8,128)(2,1)S(1)}, u32[]{:S(2)}, u32[]{:S(2)}) collective-permute-start(bf16[512,768]{0,1:T(8,128)(2,1)} %bitcast.105), channel_id=1, source_target_pairs={{0,2},{1,3},{2,0},{3,1},{4,6},{5,7},{6,4},{7,5},{8,10},{9,11},{10,... | collective-permute-start | bytes 2359304 | tf_op jit(solution)/shard_map/ppermute | solution.py:422
  9.5 85.0 %copy-start.8 = (bf16[1,512,768]{1,2,0:T(8,128)(2,1)}, bf16[1,512,768]{1,2,0:T(8,128)(2,1)S(1)}, u32[]{:S(2)}) copy-start(bf16[1,512,768]{1,2,0:T(8,128)(2,1)S(1)} %copy.53) | copy-start | bytes 2359300
  13.4 3.7 copy-start.54
  13.4 26.2 %collective-permute-start.3 = (bf16[512,768]{1,0:T(8,128)(2,1)}, bf16[512,768]{1,0:T(8,128)(2,1)}, u32[]{:S(2)}, u32[]{:S(2)}) collective-permute-start(bf16[512,768]{1,0:T(8,128)(2,1)} %add_convert_fusion.6), channel_id=1, source_target_pairs={{0,1},{1,0},{2,3},{3,2},{4,5},{5,4},{6,7},{7,6},{8,9},{9,8},{10,11... | collective-permute-start | bytes 2359304 | tf_op jit(solution)/shard_map/ppermute | solution.py:459
  15.5 28.0 %collective-permute-start.1 = (bf16[512,768]{1,0:T(8,128)(2,1)}, bf16[512,768]{1,0:T(8,128)(2,1)}, u32[]{:S(2)}, u32[]{:S(2)}) collective-permute-start(bf16[512,768]{1,0:T(8,128)(2,1)} %convolution_convert_fusion.8), channel_id=1, source_target_pairs={{0,1},{1,0},{2,3},{3,2},{4,5},{5,4},{6,7},{7,6},{8,9},{9,8},{10,11... | collective-permute-start | bytes 2359304 | tf_op jit(solution)/shard_map/ppermute | solution.py:459
  17.2 118.3 %collective-permute-start.6 = (bf16[512,768]{0,1:T(8,128)(2,1)}, bf16[512,768]{0,1:T(8,128)(2,1)}, u32[]{:S(2)}, u32[]{:S(2)}) collective-permute-start(bf16[512,768]{0,1:T(8,128)(2,1)} %bitcast.104), channel_id=1, source_target_pairs={{0,2},{1,3},{2,0},{3,1},{4,6},{5,7},{6,4},{7,5},{8,10},{9,11},{10,... | collective-permute-start | bytes 2359304 | tf_op jit(solution)/shard_map/ppermute | solution.py:422
  20.4 6.8 %copy-start.44 = (bf16[768,768]{1,0:T(8,128)(2,1)S(1)}, bf16[768,768]{1,0:T(8,128)(2,1)}, u32[]{:S(2)}) copy-start(bf16[768,768]{1,0:T(8,128)(2,1)} %param.25) | copy-start | bytes 3538948
  20.4 6.8 %copy-start.47 = (f32[768]{0:T(1024)S(1)}, f32[768]{0:T(1024)}, u32[]{:S(2)}) copy-start(f32[768]{0:T(1024)} %param.26) | copy-start | bytes 9220
  20.4 6.8 %copy-start.52 = (f32[768]{0:T(1024)S(1)}, f32[768]{0:T(1024)}, u32[]{:S(2)}) copy-start(f32[768]{0:T(1024)} %param.21) | copy-start | bytes 9220
  26.7 9.3 %copy-start.14 = (bf16[512,768]{0,1:T(8,128)(2,1)}, bf16[512,768]{0,1:T(8,128)(2,1)S(1)}, u32[]{:S(2)}) copy-start(bf16[512,768]{0,1:T(8,128)(2,1)S(1)} %collective-permute-done) | copy-start | bytes 2359300
  29.2 6.8 %copy-start.48 = (f32[768]{0:T(1024)S(1)}, f32[768]{0:T(1024)}, u32[]{:S(2)}) copy-start(f32[768]{0:T(1024)} %param.23) | copy-start | bytes 9220
  29.2 10.5 %collective-permute-start.4 = (bf16[512,768]{1,0:T(8,128)(2,1)}, bf16[512,768]{1,0:T(8,128)(2,1)}, u32[]{:S(2)}, u32[]{:S(2)}) collective-permute-start(bf16[512,768]{1,0:T(8,128)(2,1)} %add_convert_fusion.5), channel_id=1, source_target_pairs={{0,1},{1,0},{2,3},{3,2},{4,5},{5,4},{6,7},{7,6},{8,9},{9,8},{10,11... | collective-permute-start | bytes 2359304 | tf_op jit(solution)/shard_map/ppermute | solution.py:459
  31.2 12.2 %collective-permute-start.2 = (bf16[512,768]{1,0:T(8,128)(2,1)}, bf16[512,768]{1,0:T(8,128)(2,1)}, u32[]{:S(2)}, u32[]{:S(2)}) collective-permute-start(bf16[512,768]{1,0:T(8,128)(2,1)} %convolution_convert_fusion.7), channel_id=1, source_target_pairs={{0,1},{1,0},{2,3},{3,2},{4,5},{5,4},{6,7},{7,6},{8,9},{9,8},{10,11... | collective-permute-start | bytes 2359304 | tf_op jit(solution)/shard_map/ppermute | solution.py:459
  32.5 14.3 %copy-start.6 = (s32[5]{0:T(128)}, s32[5]{0:T(128)S(1)}, u32[]{:S(2)}) copy-start(s32[5]{0:T(128)S(1)} %pad_add_fusion.info_ref) | copy-start | bytes 64
  39.7 7.1 %copy-start.2 = (bf16[1024,768]{1,0:T(8,128)(2,1)}, bf16[1024,768]{1,0:T(8,128)(2,1)S(1)}, u32[]{:S(2)}) copy-start(bf16[1024,768]{1,0:T(8,128)(2,1)S(1)} %pad_maximum_fusion.4.q_ref) | copy-start | bytes 4718596
  46.8 47.8 %copy-start.15 = (bf16[512,768]{0,1:T(8,128)(2,1)S(1)}, bf16[512,768]{0,1:T(8,128)(2,1)}, u32[]{:S(2)}) copy-start(bf16[512,768]{0,1:T(8,128)(2,1)} %copy-done.14) | copy-start | bytes 2359300
  46.8 47.8 %copy-start.37 = (f32[768]{0:T(1024)S(1)}, f32[768]{0:T(1024)}, u32[]{:S(2)}) copy-start(f32[768]{0:T(1024)} %param.28) | copy-start | bytes 9220
  94.5 4.2 copy-start.4
  94.5 4.6 slice-start
  94.6 4.6 slice-start.1
  98.7 36.8 %copy-start.12 = (f32[1024,768]{0,1:T(8,128)}, f32[1024,768]{0,1:T(8,128)S(1)}, u32[]{:S(2)}) copy-start(f32[1024,768]{0,1:T(8,128)S(1)} %get-tuple-element.108) | copy-start | bytes 9437188
  99.5 36.0 %copy-start.19 = (bf16[1,512,768]{1,2,0:T(8,128)(2,1)S(1)}, bf16[1,512,768]{1,2,0:T(8,128)(2,1)}, u32[]{:S(2)}) copy-start(bf16[1,512,768]{1,2,0:T(8,128)(2,1)} %copy.56) | copy-start | bytes 2359300
  163.4 3.5 copy-start.49
  166.9 14.0 %copy-start.13 = (f32[1024,768]{0,1:T(8,128)S(1)}, f32[1024,768]{0,1:T(8,128)}, u32[]{:S(2)}) copy-start(f32[1024,768]{0,1:T(8,128)} %copy-done.12) | copy-start | bytes 9437188
  166.9 14.0 %copy-start.18 = (f32[1024,768]{0,1:T(8,128)S(1)}, f32[1024,768]{0,1:T(8,128)}, u32[]{:S(2)}) copy-start(f32[1024,768]{0,1:T(8,128)} %copy.58) | copy-start | bytes 9437188
  272.9 32.6 %collective-permute-start.7 = (bf16[1024,768]{1,0:T(8,128)(2,1)}, bf16[1024,768]{1,0:T(8,128)(2,1)}, u32[]{:S(2)}, u32[]{:S(2)}) collective-permute-start(bf16[1024,768]{1,0:T(8,128)(2,1)} %slice.101), channel_id=1, source_target_pairs={{0,1},{1,0},{2,3},{3,2},{4,5},{5,4},{6,7},{7,6},{8,9},{9,8},{10,11... | collective-permute-start | bytes 4718600 | tf_op jit(solution)/shard_map/ppermute | solution.py:510
  273.0 11.0 %slice-start.2 = ((s8[6291456]{0:T(1024)(128)(4,1)}), s8[4194304]{0:T(1024)(128)(4,1)S(1)}, s32[]{:S(2)}) async-start(s8[6291456]{0:T(1024)(128)(4,1)} %bitcast.115), calls=%async_computation.2 | async-start | bytes 8388608
  273.0 11.0 %slice-start.3 = ((s8[6291456]{0:T(1024)(128)(4,1)}), s8[2097152]{0:T(1024)(128)(4,1)S(1)}, s32[]{:S(2)}) async-start(s8[6291456]{0:T(1024)(128)(4,1)} %bitcast.115), calls=%async_computation.3 | async-start | bytes 4194304
  273.0 28.4 %collective-permute-start.5 = (bf16[512,768]{0,1:T(8,128)(2,1)S(1)}, bf16[512,768]{0,1:T(8,128)(2,1)S(1)}, u32[]{:S(2)}, u32[]{:S(2)}) collective-permute-start(bf16[512,768]{0,1:T(8,128)(2,1)S(1)} %get-tuple-element.116), channel_id=1, source_target_pairs={{0,2},{1,3},{2,0},{3,1},{4,6},{5,7},{6,4},{7,5},{8,10},{9,11},{10,... | collective-permute-start | bytes 2359304 | tf_op jit(solution)/shard_map/ppermute | solution.py:428
  284.0 7.4 %copy-start.22 = (bf16[2048,768]{1,0:T(8,128)(2,1)S(1)}, bf16[2048,768]{1,0:T(8,128)(2,1)}, u32[]{:S(2)}) copy-start(bf16[2048,768]{1,0:T(8,128)(2,1)} %get-tuple-element.38) | copy-start | bytes 9437188
  291.4 4.5 copy-start.41
  292.6 16.6 %collective-permute-start.8 = (bf16[1024,768]{1,0:T(8,128)(2,1)}, bf16[1024,768]{1,0:T(8,128)(2,1)}, u32[]{:S(2)}, u32[]{:S(2)}) collective-permute-start(bf16[1024,768]{1,0:T(8,128)(2,1)} %slice.103), channel_id=1, source_target_pairs={{0,1},{1,0},{2,3},{3,2},{4,5},{5,4},{6,7},{7,6},{8,9},{9,8},{10,11... | collective-permute-start | bytes 4718600 | tf_op jit(solution)/shard_map/ppermute | solution.py:510
  305.4 3.9 copy-start.9
  305.4 3.9 copy-start.16
  305.4 3.9 copy-start.23
  305.4 3.9 copy-start.34
  305.4 4.0 copy-start.45
  305.5 5.0 %copy-start.55 = (f32[1024,768]{0,1:T(8,128)S(1)}, f32[1024,768]{0,1:T(8,128)}, u32[]{:S(2)}) copy-start(f32[1024,768]{0,1:T(8,128)} %fusion.61) | copy-start | bytes 9437188
  314.1 3.9 copy-start.17
  314.1 3.9 copy-start.40
  314.1 4.0 copy-start.36
  314.1 4.0 copy-start.39
  314.1 4.6 copy-start.53
  430.3 9.1 %copy-start.11 = (f32[1024,768]{0,1:T(8,128)S(1)}, f32[1024,768]{0,1:T(8,128)}, u32[]{:S(2)}) copy-start(f32[1024,768]{0,1:T(8,128)} %copy-done.10) | copy-start | bytes 9437188
  430.3 9.1 %copy-start.21 = (bf16[1,512,768]{1,2,0:T(8,128)(2,1)S(1)}, bf16[1,512,768]{1,2,0:T(8,128)(2,1)}, u32[]{:S(2)}) copy-start(bf16[1,512,768]{1,2,0:T(8,128)(2,1)} %copy.56) | copy-start | bytes 2359300
  442.9 19.9 %collective-permute-start.9 = (bf16[512,768]{0,1:T(8,128)(2,1)S(1)}, bf16[512,768]{0,1:T(8,128)(2,1)S(1)}, u32[]{:S(2)}, u32[]{:S(2)}) collective-permute-start(bf16[512,768]{0,1:T(8,128)(2,1)S(1)} %get-tuple-element.111), channel_id=1, source_target_pairs={{0,2},{1,3},{2,0},{3,1},{4,6},{5,7},{6,4},{7,5},{8,10},{9,11},{10,... | collective-permute-start | bytes 2359304 | tf_op jit(solution)/shard_map/ppermute | solution.py:428
  (22 other events, 43.3 us)
